TPU v7x, 32 devices: a whole 2x2x4 slice. The times are simulated.
32 devices in a mesh: tile: 8 (over y, x, core), chan: 4 (over z).
Axes of the slice: x: 2, y: 2, z: 4, core: 2. Of those that a mesh axis runs over, the one named last changes fastest.
Arguments:
- ensemble: bfloat16 [3072, 128, 256], P('tile', 'chan'), may hold values from -6 to 6
- jacobian: bfloat16 [1280, 128, 128], P('tile', 'chan'), may hold values from -1 to 1
- innovation: float32 [1280, 128], P('tile', 'chan'), may hold values from -6 to 6
- error_vectors: float32 [128, 32], replicated, may hold values from -1 to 1, as said below
- error_values: float32 [128], replicated, may hold values from 0.25 to 4
- ensemble_vectors: float32 [256, 256], replicated, may hold values from -1 to 1, as said below
- column_pick: int32 [8, 5, 40], P('tile'), may hold values from 0 to 383
- footprint_slot: int32 [1280], P('tile'), may hold values from 0 to 199, as said below
- footprint_count: int32 [8], P('tile'), may hold values from 20 to 160, as said below
Outputs:
- analysis: bfloat16 [3072, 128, 256], P('tile', 'chan')
Inputs may be any that keep to these rules, and one draw needn't show every extreme that they name: `footprint_slot`: the 160 entries of one pack are distinct; slot o * 40 + j is the j-th column that tile (pack + 2 - o) mod 8 sends to this pack. `footprint_count`: some pack has all 160 footprints live. `error_vectors`: each block of 32 rows is an orthogonal matrix. `ensemble_vectors`: an orthogonal matrix.
All inputs are finite; a program needn't handle non-finite values.
Results may differ from a plain program's by a relative error of at most 0.013.
Values may be sent and summed in bfloat16 or wider, within the bound.
A program may use at most 64 MiB of HBM per device.

v0:
```python
import jax
import jax.numpy as jnp
from jax import lax
from jax.sharding import PartitionSpec as P


def from_behind(value, axis, steps):
    count = lax.axis_size(axis)
    pairs = [(source, (source + steps) % count) for source in range(count)]
    return lax.ppermute(value, axis, pairs)


def turn_blocks(values, vectors):
    row_count, channels, members = values.shape
    group_width = vectors.shape[1]
    grouped = values.reshape(row_count, channels // group_width, group_width, members)
    basis_blocks = vectors.reshape(channels // group_width, group_width, group_width)
    turned = jnp.einsum("gce,fgck->fgek", basis_blocks, grouped, precision=lax.Precision.HIGHEST)
    return turned.reshape(row_count, channels, members)


def turn_rows(values, vectors):
    row_count, channels = values.shape
    group_width = vectors.shape[1]
    grouped = values.reshape(row_count, channels // group_width, group_width)
    basis_blocks = vectors.reshape(channels // group_width, group_width, group_width)
    turned = jnp.einsum("gce,fgc->fge", basis_blocks, grouped, precision=lax.Precision.HIGHEST)
    return turned.reshape(row_count, channels)


def local(
    ensemble,
    jacobian,
    innovation,
    error_vectors,
    error_values,
    ensemble_vectors,
    column_pick,
    footprint_slot,
    footprint_count,
):
    window = column_pick.shape[1]
    capacity = column_pick.shape[2]
    reach_tiles = window // 2
    level_part = ensemble.shape[1]
    members = ensemble.shape[2]
    chosen = jnp.take(ensemble, column_pick[0].reshape(-1), axis=0).reshape(
        window, capacity, level_part, members
    )
    blocks = []
    for slot_index in range(window):
        shift_by = slot_index - reach_tiles
        if shift_by == 0:
            blocks.append(chosen[slot_index])
        else:
            blocks.append(from_behind(chosen[slot_index], "tile", shift_by))
    arrived = jnp.stack(blocks, 0)
    slot_rows = arrived.reshape(window * capacity, level_part, members)
    columns = jnp.take(slot_rows, footprint_slot, axis=0)
    foot_rows = columns.shape[0]
    live_rows = (jnp.arange(foot_rows, dtype=jnp.int32) < footprint_count[0]).astype(jnp.float32)
    share_rows = foot_rows // lax.axis_size("chan")
    columns, sensitivity, misfit_rows = (
        lax.all_to_all(columns, "chan", split_axis=0, concat_axis=1, tiled=True),
        lax.all_to_all(jacobian, "chan", split_axis=0, concat_axis=1, tiled=True),
        lax.all_to_all(
            innovation.astype(jnp.bfloat16), "chan", split_axis=0, concat_axis=1, tiled=True
        ).astype(innovation.dtype),
    )
    response = jnp.einsum("fcl,flk->fck", sensitivity, columns, preferred_element_type=jnp.float32)
    row_weights = lax.dynamic_slice_in_dim(
        live_rows, lax.axis_index("chan") * share_rows, share_rows, 0
    )
    scales = 1.0 / jnp.sqrt(error_values)
    whitened = (
        turn_blocks(response, error_vectors) * scales[None, :, None] * row_weights[:, None, None]
    )
    misfit = turn_rows(misfit_rows, error_vectors) * scales[None, :]
    pull_sum = jnp.einsum("fck,fc->k", whitened, misfit, precision=lax.Precision.HIGHEST)
    rounded = whitened.astype(jnp.bfloat16).reshape(-1, members)
    gram_sum = lax.dot_general(
        rounded, rounded, (((0,), (0,)), ((), ())), preferred_element_type=jnp.float32
    )
    gram_sum, pull_sum = lax.psum((gram_sum, pull_sum), ("tile", "chan"))
    system = gram_sum + (members - 1) * jnp.eye(members, dtype=jnp.float32)
    factor = jnp.linalg.cholesky(system)
    halfway = lax.linalg.triangular_solve(factor, pull_sum[:, None], left_side=True, lower=True)
    mean_weights = lax.linalg.triangular_solve(
        factor, halfway, left_side=True, lower=True, transpose_a=True
    )[:, 0]
    spread = jnp.sqrt(members - 1.0) * lax.linalg.triangular_solve(
        factor, ensemble_vectors, left_side=True, lower=True, transpose_a=True
    )
    transform = (spread + mean_weights[:, None]).astype(jnp.bfloat16)
    flat_rows = ensemble.reshape(-1, members)
    updated = jnp.dot(flat_rows, transform, preferred_element_type=jnp.float32).astype(jnp.bfloat16)
    return updated.reshape(ensemble.shape)


def solution(mesh):
    return jax.shard_map(
        local,
        mesh=mesh,
        in_specs=(
            P("tile", "chan", None),
            P("tile", "chan", None),
            P("tile", "chan"),
            P(),
            P(),
            P(),
            P("tile", None, None),
            P("tile"),
            P("tile"),
        ),
        out_specs=P("tile", "chan", None),
        check_vma=False,
    )
```

profile of v0, /device:TPU:0, one launch (start us, length us, event | category | flops | bytes accessed | tf_op | source)
XLA Modules:
  0.0 357.7 jit_solution(7432755867193582582)
XLA Ops:
  7.4 5.5 %gather_fusion = bf16[200,32,256]{2,1,0:T(8,128)(2,1)} fusion(bf16[384,32,256]{2,1,0:T(8,128)(2,1)} %param.9, s32[1024]{0:T(1024)S(1)} %pad_clamp_fusion.1), kind=kCustom, calls=%fused_computation | custom fusion | bytes 6554400 | tf_op jit(solution)/shard_map/jit(_take)/gather | solution.py:47
  12.9 2.3 broadcast_select_fusion
  16.8 3.9 %collective-permute-start = (bf16[40,32,256]{2,1,0:T(8,128)(2,1)}, bf16[40,32,256]{2,1,0:T(8,128)(2,1)}, u32[]{:S(2)}, u32[]{:S(2)}) collective-permute-start(bf16[40,32,256]{2,1,0:T(8,128)(2,1)} %get-tuple-element.34), channel_id=1, source_target_pairs={{0,24},{4,28},{8,0},{12,4},{16,8},{20,12},{24,16},{28,20},{1,25},{... | collective-permute-start | bytes 1966088 | tf_op jit(solution)/shard_map/ppermute | solution.py:10
  22.7 4.9 %all-to-all-start.2 = ((bf16[4,2,640]{2,1,0:T(2,128)(2,1)}), bf16[4,2,640]{2,1,0:T(2,128)(2,1)S(1)}, u32[]{:S(2)}, u32[]{:S(2)}) async-start(bf16[4,2,640]{2,1,0:T(2,128)(2,1)} %reshape.193), calls=%async_computation.2 | async-start | bytes 20480 | tf_op jit(solution)/shard_map/all_to_all | solution.py:66
  27.6 5.6 %all-to-all-done.2 = bf16[4,2,640]{2,1,0:T(2,128)(2,1)S(1)} async-done(((bf16[4,2,640]{2,1,0:T(2,128)(2,1)}), bf16[4,2,640]{2,1,0:T(2,128)(2,1)S(1)}, u32[]{:S(2)}, u32[]{:S(2)}) %all-to-all-start.2) | async-done | bytes 10272 | tf_op jit(solution)/shard_map/all_to_all | solution.py:66
  33.2 4.3 %all-to-all-start.1 = ((bf16[160,32,128]{2,1,0:T(8,128)(2,1)}), bf16[160,32,128]{2,1,0:T(8,128)(2,1)}, u32[]{:S(2)}, u32[]{:S(2)}) async-start(bf16[160,32,128]{2,1,0:T(8,128)(2,1)} %param.10), calls=%async_computation.1 | async-start | bytes 2621440 | tf_op jit(solution)/shard_map/all_to_all | solution.py:65
  38.7 11.5 %collective-permute-done.1 = bf16[40,32,256]{2,1,0:T(8,128)(2,1)} collective-permute-done((bf16[40,32,256]{2,1,0:T(8,128)(2,1)}, bf16[40,32,256]{2,1,0:T(8,128)(2,1)}, u32[]{:S(2)}, u32[]{:S(2)}) %collective-permute-start.1) | collective-permute-done | bytes 655392 | tf_op jit(solution)/shard_map/ppermute | solution.py:10
  52.5 11.6 %collective-permute-done.3 = bf16[40,32,256]{2,1,0:T(8,128)(2,1)} collective-permute-done((bf16[40,32,256]{2,1,0:T(8,128)(2,1)}, bf16[40,32,256]{2,1,0:T(8,128)(2,1)}, u32[]{:S(2)}, u32[]{:S(2)}) %collective-permute-start.3) | collective-permute-done | bytes 655392 | tf_op jit(solution)/shard_map/ppermute | solution.py:10
  67.0 2.7 gather_fusion.1
  71.5 5.0 %all-to-all-start = ((bf16[160,32,256]{2,1,0:T(8,128)(2,1)}), bf16[160,32,256]{2,1,0:T(8,128)(2,1)S(1)}, u32[]{:S(2)}, u32[]{:S(2)}) async-start(bf16[160,32,256]{2,1,0:T(8,128)(2,1)} %broadcast_select_fusion.1), calls=%async_computation | async-start | bytes 5242880 | tf_op jit(solution)/shard_map/all_to_all | solution.py:64
  77.9 2.8 copy.24
  80.7 54.4 %all-to-all-done = bf16[160,32,256]{2,1,0:T(8,128)(2,1)S(1)} async-done(((bf16[160,32,256]{2,1,0:T(8,128)(2,1)}), bf16[160,32,256]{2,1,0:T(8,128)(2,1)S(1)}, u32[]{:S(2)}, u32[]{:S(2)}) %all-to-all-start) | async-done | bytes 2621472 | tf_op jit(solution)/shard_map/all_to_all | solution.py:64
  137.3 6.6 %multiply_convert_fusion = (bf16[40,4,32,256]{3,2,0,1:T(8,128)(2,1)S(1)}, f32[40,4,32,256]{3,2,0,1:T(8,128)}) fusion(f32[40]{0:T(128)S(1)} %dynamic_slice.3, f32[4,32]{1,0:T(4,128)S(1)} %mul.53, f32[4,32,32,1]{1,0,2,3:T(4,128)S(1)} %bitcast.144, f32[40,4,32,256]{3,2,1,0:T(8,128)S(1)} %bitcast.138), kind=kOutput, calls=%fused_computation.10 | convolution fusion | flops 507248640 | bytes 13124256 | tf_op jit(solution)/shard_map/gce,fgck->fgek/dot_general | solution.py:18
  145.8 2.9 copy.35
  149.8 2.7 fusion.45
  152.5 37.0 %psum.15 = f32[256]{0:T(256)S(1)} all-reduce(f32[256]{0:T(256)S(1)} %bitcast.148), channel_id=1, replica_groups=mesh['tile'=8,'chan'=4] {'tile','chan'}, use_global_device_ids=true, to_apply=%region_5.6 | all-reduce | flops 256 | bytes 2048 | tf_op jit(solution)/shard_map/psum | solution.py:84
  189.5 81.2 %all-reduce.3.cloned.1.call-done = f32[256,256]{0,1:T(8,128)} async-done(((f32[256,256]{0,1:T(8,128)}), f32[256,256]{0,1:T(8,128)}) %all-reduce.3.cloned.1.call-update) | async-done | bytes 262160 | tf_op jit(solution)/shard_map/psum | solution.py:84
  272.8 11.7 %cholesky.49 = f32[128,128]{1,0:T(8,128)S(1)} custom-call(f32[128,128]{1,0:T(8,128)S(1)} %cholesky.115), custom_call_target="Cholesky" | custom-call | tf_op jit(solution)/shard_map/jit(cholesky)/cholesky | solution.py:86
  284.5 9.8 %custom-call.18 = f32[1,128,128]{1,2,0:T(8,128)S(1)} custom-call(f32[1,128,128]{2,1,0:T(8,128)S(1)} %get-tuple-element.36), custom_call_target="InvertDiagBlocksLowerTriangular" | custom-call | tf_op jit(solution)/shard_map/jit(cholesky)/cholesky | solution.py:86
  294.8 11.7 %cholesky.103 = f32[128,128]{1,0:T(8,128)S(1)} custom-call(f32[128,128]{1,0:T(8,128)S(1)} %convolution_subtract_fusion.1), custom_call_target="Cholesky" | custom-call | tf_op jit(solution)/shard_map/jit(cholesky)/cholesky | solution.py:86
  308.9 4.0 %while.1 = (s32[]{:T(128)}, f32[256,256]{0,1:T(8,128)S(1)}, s32[2,2]{1,0:T(2,128)S(1)}, f32[2,128,128]{2,1,0:T(8,128)S(1)}, s32[]{:T(128)}) while((s32[]{:T(128)}, f32[256,256]{0,1:T(8,128)S(1)}, s32[2,2]{1,0:T(2,128)S(1)}, f32[2,128,128]{2,1,0:T(8,128)S(1)}, s32[]{:T(128)}) %tuple.27), condition=%wide.while_cond, body=%wide.while_body.sunk | while | flops 2 | bytes 393321 | solution.py:91
  312.9 19.9 %custom-call.19 = f32[2,128,128]{1,2,0:T(8,128)S(1)} custom-call(f32[2,128,128]{2,1,0:T(8,128)S(1)} %get-tuple-element.12), custom_call_target="InvertDiagBlocksLowerTriangular" | custom-call | tf_op jit(solution)/shard_map/triangular_solve | solution.py:91
  334.9 7.4 %fusion = bf16[12288,256]{0,1:T(8,128)(2,1)} fusion(bf16[12288,256]{1,0:T(8,128)(2,1)} %bitcast.139, f32[128,256]{1,0:T(8,128)S(1)} %fusion.23, f32[128,256]{1,0:T(8,128)S(1)} %fusion.32, f32[256]{0:T(256)S(1)} %bitcast.147), kind=kOutput, calls=%fused_computation.5 | convolution fusion | flops 1614020608 | bytes 12846080 | tf_op jit(solution)/shard_map/dot_general | solution.py:96
  342.3 8.6 %copy.38 = bf16[12288,256]{1,0:T(8,128)(2,1)} copy(bf16[12288,256]{0,1:T(8,128)(2,1)} %fusion) | data formatting | bytes 12582912 | tf_op jit(solution)/shard_map/convert_element_type | solution.py:96
  (94 shorter events, 27.9 us)
Async XLA Ops:
  15.2 6.7 %copy-start.3 = (f32[160,32]{0,1:T(8,128)S(1)}, f32[160,32]{0,1:T(8,128)}, u32[]{:S(2)}) copy-start(f32[160,32]{0,1:T(8,128)} %param.11) | copy-start | bytes 61444
  15.3 12.4 %copy-start.5 = (s32[160]{0:T(256)S(1)}, s32[160]{0:T(256)}, u32[]{:S(2)}) copy-start(s32[160]{0:T(256)} %param.16) | copy-start | bytes 1924
  16.8 20.7 %collective-permute-start = (bf16[40,32,256]{2,1,0:T(8,128)(2,1)}, bf16[40,32,256]{2,1,0:T(8,128)(2,1)}, u32[]{:S(2)}, u32[]{:S(2)}) collective-permute-start(bf16[40,32,256]{2,1,0:T(8,128)(2,1)} %get-tuple-element.34), channel_id=1, source_target_pairs={{0,24},{4,28},{8,0},{12,4},{16,8},{20,12},{24,16},{28,20},{1,25},{... | collective-permute-start | bytes 1966088 | tf_op jit(solution)/shard_map/ppermute | solution.py:10
  20.7 29.5 %collective-permute-start.1 = (bf16[40,32,256]{2,1,0:T(8,128)(2,1)}, bf16[40,32,256]{2,1,0:T(8,128)(2,1)}, u32[]{:S(2)}, u32[]{:S(2)}) collective-permute-start(bf16[40,32,256]{2,1,0:T(8,128)(2,1)} %get-tuple-element.33), channel_id=1, source_target_pairs={{0,28},{4,0},{8,4},{12,8},{16,12},{20,16},{24,20},{28,24},{1,29},{... | collective-permute-start | bytes 1966088 | tf_op jit(solution)/shard_map/ppermute | solution.py:10
  20.7 30.7 %collective-permute-start.2 = (bf16[40,32,256]{2,1,0:T(8,128)(2,1)}, bf16[40,32,256]{2,1,0:T(8,128)(2,1)}, u32[]{:S(2)}, u32[]{:S(2)}) collective-permute-start(bf16[40,32,256]{2,1,0:T(8,128)(2,1)} %get-tuple-element.32), channel_id=1, source_target_pairs={{0,4},{4,8},{8,12},{12,16},{16,20},{20,24},{24,28},{28,0},{1,5},{5... | collective-permute-start | bytes 1966088 | tf_op jit(solution)/shard_map/ppermute | solution.py:10
  21.2 42.9 %collective-permute-start.3 = (bf16[40,32,256]{2,1,0:T(8,128)(2,1)}, bf16[40,32,256]{2,1,0:T(8,128)(2,1)}, u32[]{:S(2)}, u32[]{:S(2)}) collective-permute-start(bf16[40,32,256]{2,1,0:T(8,128)(2,1)} %get-tuple-element.31), channel_id=1, source_target_pairs={{0,8},{4,12},{8,16},{12,20},{16,24},{20,28},{24,0},{28,4},{1,9},{5... | collective-permute-start | bytes 1966088 | tf_op jit(solution)/shard_map/ppermute | solution.py:10
  22.7 10.5 %all-to-all-start.2 = ((bf16[4,2,640]{2,1,0:T(2,128)(2,1)}), bf16[4,2,640]{2,1,0:T(2,128)(2,1)S(1)}, u32[]{:S(2)}, u32[]{:S(2)}) async-start(bf16[4,2,640]{2,1,0:T(2,128)(2,1)} %reshape.193), calls=%async_computation.2 | async-start | bytes 20480 | tf_op jit(solution)/shard_map/all_to_all | solution.py:66
  33.2 38.3 %all-to-all-start.1 = ((bf16[160,32,128]{2,1,0:T(8,128)(2,1)}), bf16[160,32,128]{2,1,0:T(8,128)(2,1)}, u32[]{:S(2)}, u32[]{:S(2)}) async-start(bf16[160,32,128]{2,1,0:T(8,128)(2,1)} %param.10), calls=%async_computation.1 | async-start | bytes 2621440 | tf_op jit(solution)/shard_map/all_to_all | solution.py:65
  65.2 1.7 copy-start.1
  71.5 5.7 %copy-start.6 = (f32[128]{0:T(128)S(1)}, f32[128]{0:T(128)}, u32[]{:S(2)}) copy-start(f32[128]{0:T(128)} %param.13) | copy-start | bytes 1540
  71.5 5.8 %copy-start.4 = (f32[128,32]{0,1:T(8,128)S(1)}, f32[128,32]{0,1:T(8,128)}, u32[]{:S(2)}) copy-start(f32[128,32]{0,1:T(8,128)} %param.12) | copy-start | bytes 49156
  71.5 63.6 %all-to-all-start = ((bf16[160,32,256]{2,1,0:T(8,128)(2,1)}), bf16[160,32,256]{2,1,0:T(8,128)(2,1)S(1)}, u32[]{:S(2)}, u32[]{:S(2)}) async-start(bf16[160,32,256]{2,1,0:T(8,128)(2,1)} %broadcast_select_fusion.1), calls=%async_computation | async-start | bytes 5242880 | tf_op jit(solution)/shard_map/all_to_all | solution.py:64
  76.5 194.1 %all-reduce.3.cloned.1.call-start = ((), (), s32[]{:S(2)}) async-start(), calls=%async_computation.3 | async-start | bytes 524288 | tf_op jit(solution)/shard_map/psum | solution.py:84
  135.1 1.3 copy-start
  189.5 144.6 %copy-start.2 = (f32[256,256]{1,0:T(8,128)S(1)}, f32[256,256]{1,0:T(8,128)}, u32[]{:S(2)}) copy-start(f32[256,256]{1,0:T(8,128)} %param.14) | copy-start | bytes 786436
Sparse Core Ops, SparseCore 0:
  145.9 124.6 all-reduce.2
where the time goes:
time: 359 us; the launch traced here: 358 us
  waiting for transfers between devices  164 us (46%)
  other arithmetic  61.9 us (17%)
  local copies, waits for them, and re-layouts  37.6 us (10%)
  blocking collectives  37 us (10%)
  matrix products  21.9 us (6%)
  starting transfers between devices  19.3 us (5%)
  between operations  15.6 us (4%)
    psum x1, waiting for transfers between devices, local(): gram_sum, pull_sum = lax.psum((gram_sum, pull_sum), ('tile', 'chan'))  81.2 us
    all_to_all x1, waiting for transfers between devices, local(): lax.all_to_all(columns, 'chan', split_axis=0, concat_axis=1, tiled=True)  54.4 us
    psum x1, blocking collectives, local(): gram_sum, pull_sum = lax.psum((gram_sum, pull_sum), ('tile', 'chan'))  37 us
    another operation x6, other arithmetic, local(): factor = jnp.linalg.cholesky(system)  33.9 us
    ppermute x4, waiting for transfers between devices, from_behind(): return lax.ppermute(value, axis, pairs)  23.1 us
    another operation x3, other arithmetic, local(): lax.linalg.triangular_solve(factor, ensemble_vectors, left_side=True, low...  20 us
    convert_element_type x1, local copies, waits for them, and re-layouts, local(): jnp.dot(flat_rows, transform, preferred_element_type=jnp.float32)  8.6 us
    dot_general x1, matrix products, local(): jnp.dot(flat_rows, transform, preferred_element_type=jnp.float32)  7.38 us
  transfers between devices with their start and end apart: 8, of which 5 were waited for; matrix products, arithmetic and copies ran while one was open for 6% of the time, Pallas kernels for 0%

commit v1 on v0

--- a/solution.py
+++ b/solution.py
@@ -1,7 +1,162 @@
+import functools
 import jax
 import jax.numpy as jnp
 from jax import lax
+from jax.experimental import pallas as pl
+from jax.experimental.pallas import tpu as pltpu
 from jax.sharding import PartitionSpec as P
+
+MESH = pl.DeviceIdType.MESH
+
+
+def greet(axes):
+    barrier = pltpu.get_barrier_semaphore()
+    total = 0
+    for axis in axes:
+        count = lax.axis_size(axis)
+        here = lax.axis_index(axis)
+        for step in range(1, count):
+            pl.semaphore_signal(
+                barrier, inc=1, device_id={axis: lax.rem(here + step, count)}, device_id_type=MESH
+            )
+        total += count - 1
+    pl.semaphore_wait(barrier, total)
+
+
+def sum_kernel(piece, x_ref, out_ref, landed, crossed, mine, summed, spread, sems_a, sems_b, sems_c):
+    tiles = lax.axis_size("tile")
+    chans = lax.axis_size("chan")
+    tile = lax.axis_index("tile")
+    chan = lax.axis_index("chan")
+    greet(("tile", "chan"))
+
+    def rows_of(index):
+        return pl.ds(pl.multiple_of(index * piece, 8), piece)
+
+    copies = []
+    for step in range(1, tiles):
+        peer = lax.rem(tile + step, tiles)
+        copies.append(
+            pltpu.make_async_remote_copy(
+                src_ref=x_ref.at[rows_of(peer)],
+                dst_ref=landed.at[step],
+                send_sem=sems_a.at[0, step],
+                recv_sem=sems_a.at[1, step],
+                device_id={"tile": peer},
+                device_id_type=MESH,
+            )
+        )
+    for copy in copies:
+        copy.start()
+    total = x_ref[rows_of(tile), :]
+    for step, copy in enumerate(copies, 1):
+        copy.wait_recv()
+        total = total + landed[step]
+    mine[...] = total
+    crossings = []
+    for step in range(1, chans):
+        crossings.append(
+            pltpu.make_async_remote_copy(
+                src_ref=mine,
+                dst_ref=crossed.at[step],
+                send_sem=sems_b.at[0, step],
+                recv_sem=sems_b.at[1, step],
+                device_id={"chan": lax.rem(chan + step, chans)},
+                device_id_type=MESH,
+            )
+        )
+    for copy in crossings:
+        copy.start()
+    for step, copy in enumerate(crossings, 1):
+        copy.wait_recv()
+        total = total + crossed[step]
+    summed[...] = total
+    shares = []
+    for step in range(1, tiles):
+        shares.append(
+            pltpu.make_async_remote_copy(
+                src_ref=summed,
+                dst_ref=spread.at[step],
+                send_sem=sems_c.at[0, step],
+                recv_sem=sems_c.at[1, step],
+                device_id={"tile": lax.rem(tile + step, tiles)},
+                device_id_type=MESH,
+            )
+        )
+    for copy in shares:
+        copy.start()
+    out_ref[rows_of(tile), :] = total
+    for step, copy in enumerate(shares, 1):
+        copy.wait_recv()
+        out_ref[rows_of(lax.rem(tile - step + tiles, tiles)), :] = spread[step]
+    for copy in copies + crossings + shares:
+        copy.wait_send()
+
+
+def sum_all(gram, pull):
+    tiles = lax.axis_size("tile")
+    chans = lax.axis_size("chan")
+    members = gram.shape[0]
+    half = members // 2
+    used = 3 * half + 8
+    piece = -(-used // (8 * tiles)) * 8
+    flat = jnp.concatenate(
+        [
+            gram[:half, :half],
+            gram[:half, half:],
+            gram[half:, half:],
+            pull.reshape(2, half),
+            jnp.zeros((piece * tiles - 3 * half - 2, half), jnp.float32),
+        ],
+        0,
+    )
+    out = pl.pallas_call(
+        functools.partial(sum_kernel, piece),
+        out_shape=jax.ShapeDtypeStruct(flat.shape, jnp.float32),
+        in_specs=[pl.BlockSpec(memory_space=pltpu.VMEM)],
+        out_specs=pl.BlockSpec(memory_space=pltpu.VMEM),
+        scratch_shapes=[
+            pltpu.VMEM((tiles, piece, half), jnp.float32),
+            pltpu.VMEM((chans, piece, half), jnp.float32),
+            pltpu.VMEM((piece, half), jnp.float32),
+            pltpu.VMEM((piece, half), jnp.float32),
+            pltpu.VMEM((tiles, piece, half), jnp.float32),
+            pltpu.SemaphoreType.DMA((2, tiles)),
+            pltpu.SemaphoreType.DMA((2, chans)),
+            pltpu.SemaphoreType.DMA((2, tiles)),
+        ],
+        compiler_params=pltpu.CompilerParams(collective_id=0, has_side_effects=True),
+        name="sum_all",
+    )(flat)
+    top = out[:half]
+    across = out[half : 2 * half]
+    low = out[2 * half : 3 * half]
+    gram = jnp.concatenate(
+        [jnp.concatenate([top, across], 1), jnp.concatenate([across.T, low], 1)], 0
+    )
+    return gram, out[3 * half : 3 * half + 2].reshape(members)
+
+
+def apply_kernel(x_ref, w_ref, o_ref):
+    o_ref[...] = jnp.dot(x_ref[...], w_ref[...], preferred_element_type=jnp.float32).astype(o_ref.dtype)
+
+
+def apply_transform(rows, transform):
+    count, members = rows.shape
+    block = min(count, 2048)
+    while count % block:
+        block //= 2
+    return pl.pallas_call(
+        apply_kernel,
+        grid=(count // block,),
+        out_shape=jax.ShapeDtypeStruct(rows.shape, rows.dtype),
+        in_specs=[
+            pl.BlockSpec((block, members), lambda i: (i, 0)),
+            pl.BlockSpec((members, members), lambda i: (0, 0)),
+        ],
+        out_specs=pl.BlockSpec((block, members), lambda i: (i, 0)),
+        name="apply_transform",
+    )(rows, transform)
 
 
 def from_behind(value, axis, steps):
@@ -81,7 +236,7 @@
     gram_sum = lax.dot_general(
         rounded, rounded, (((0,), (0,)), ((), ())), preferred_element_type=jnp.float32
     )
-    gram_sum, pull_sum = lax.psum((gram_sum, pull_sum), ("tile", "chan"))
+    gram_sum, pull_sum = sum_all(gram_sum, pull_sum)
     system = gram_sum + (members - 1) * jnp.eye(members, dtype=jnp.float32)
     factor = jnp.linalg.cholesky(system)
     halfway = lax.linalg.triangular_solve(factor, pull_sum[:, None], left_side=True, lower=True)
@@ -93,7 +248,7 @@
     )
     transform = (spread + mean_weights[:, None]).astype(jnp.bfloat16)
     flat_rows = ensemble.reshape(-1, members)
-    updated = jnp.dot(flat_rows, transform, preferred_element_type=jnp.float32).astype(jnp.bfloat16)
+    updated = apply_transform(flat_rows, transform)
     return updated.reshape(ensemble.shape)
 
 

time: 359 us -> 248 us (0.69)
  waiting for transfers between devices: 164 us -> 83 us
  blocking collectives: 37 us -> 0 us
  Pallas kernels: 0 us -> 23.6 us
  between operations: 15.6 us -> 2.39 us
  matrix products: 21.9 us -> 11.1 us
  other arithmetic: 61.9 us -> 71.9 us
    psum x1 -> x0, waiting for transfers between devices: 81.2 us -> none  [local(): gram_sum, pull_sum = lax.psum((gram_sum, pull_sum), ('tile', 'chan'))]
    psum x1 -> x0, blocking collectives: 37 us -> none  [local(): gram_sum, pull_sum = lax.psum((gram_sum, pull_sum), ('tile', 'chan'))]
    pallas_call x0 -> x2, Pallas kernels: none -> 23.6 us  [the longest x1 15.6 us: sum_all(): pl.pallas_call(functools.partial(sum_kernel, piece), out_shape=jax.ShapeD...]
    dot_general x2 -> x0, matrix products: 10 us -> none  [the longest x1 7.38 us: local(): jnp.dot(flat_rows, transform, preferred_element_type=jnp.float32)]
    convert_element_type x1 -> x0, local copies, waits for them, and re-layouts: 8.6 us -> none  [local(): jnp.dot(flat_rows, transform, preferred_element_type=jnp.float32)]
    dot_general x0 -> x1, local copies, waits for them, and re-layouts: none -> 7.71 us  [local(): jnp.einsum('fck,fc->k', whitened, misfit, precision=lax.Precision.HIGHEST)]
    dot_general x0 -> x1, other arithmetic: none -> 7.54 us  [local(): jnp.einsum('fck,fc->k', whitened, misfit, precision=lax.Precision.HIGHEST)]
    unnamed x20 -> x24, local copies, waits for them, and re-layouts: 7.04 us -> 7.2 us
  transfers between devices with their start and end apart: 8 -> 7, of which waited for: 5 -> 4; matrix products, arithmetic and copies ran while one was open for 6% -> 5% of each run, Pallas kernels for 0% -> 0%
where the time goes in v1:
time: 248 us; the launch traced here: 247 us
  waiting for transfers between devices  83 us (33%)
  other arithmetic  71.9 us (29%)
  local copies, waits for them, and re-layouts  36 us (15%)
  Pallas kernels  23.6 us (10%)
  starting transfers between devices  19.3 us (8%)
  matrix products  11.1 us (4%)
    all_to_all x1, waiting for transfers between devices, local(): lax.all_to_all(columns, 'chan', split_axis=0, concat_axis=1, tiled=True)  54.3 us
    another operation x6, other arithmetic, local(): factor = jnp.linalg.cholesky(system)  34 us
    ppermute x4, waiting for transfers between devices, from_behind(): return lax.ppermute(value, axis, pairs)  23.1 us
    another operation x3, other arithmetic, local(): lax.linalg.triangular_solve(factor, ensemble_vectors, left_side=True, low...  20 us
    pallas_call x1, Pallas kernels, sum_all(): pl.pallas_call(functools.partial(sum_kernel, piece), out_shape=jax.ShapeD...  15.6 us
    pallas_call x1, Pallas kernels, apply_transform(): pl.pallas_call(apply_kernel, grid=(count // block,), out_shape=jax.ShapeD...  7.93 us
    dot_general x1, local copies, waits for them, and re-layouts, local(): jnp.einsum('fck,fc->k', whitened, misfit, precision=lax.Precision.HIGHEST)  7.71 us
    dot_general x1, other arithmetic, local(): jnp.einsum('fck,fc->k', whitened, misfit, precision=lax.Precision.HIGHEST)  7.54 us
  transfers between devices with their start and end apart: 7, of which 4 were waited for; matrix products, arithmetic and copies ran while one was open for 5% of the time, Pallas kernels for 0%

profile of v1, /device:TPU:0, one launch (start us, length us, event | category | flops | bytes accessed | tf_op | source)
XLA Modules:
  0.0 247.2 jit_solution(7800314165887166224)
XLA Ops:
  0.9 5.5 %gather_fusion = bf16[200,32,256]{2,1,0:T(8,128)(2,1)} fusion(bf16[384,32,256]{2,1,0:T(8,128)(2,1)} %param.9, s32[1024]{0:T(1024)S(1)} %pad_clamp_fusion.1), kind=kCustom, calls=%fused_computation | custom fusion | bytes 6554400 | tf_op jit(solution)/shard_map/jit(_take)/gather | solution.py:202
  6.4 2.3 broadcast_select_fusion
  10.3 3.9 %collective-permute-start = (bf16[40,32,256]{2,1,0:T(8,128)(2,1)}, bf16[40,32,256]{2,1,0:T(8,128)(2,1)}, u32[]{:S(2)}, u32[]{:S(2)}) collective-permute-start(bf16[40,32,256]{2,1,0:T(8,128)(2,1)} %get-tuple-element.34), channel_id=1, source_target_pairs={{0,24},{4,28},{8,0},{12,4},{16,8},{20,12},{24,16},{28,20},{1,25},{... | collective-permute-start | bytes 1966088 | tf_op jit(solution)/shard_map/ppermute | solution.py:165
  16.2 4.9 %all-to-all-start.2 = ((bf16[4,2,640]{2,1,0:T(2,128)(2,1)}), bf16[4,2,640]{2,1,0:T(2,128)(2,1)S(1)}, u32[]{:S(2)}, u32[]{:S(2)}) async-start(bf16[4,2,640]{2,1,0:T(2,128)(2,1)} %reshape.199), calls=%async_computation.2 | async-start | bytes 20480 | tf_op jit(solution)/shard_map/all_to_all | solution.py:221
  21.1 5.6 %all-to-all-done.2 = bf16[4,2,640]{2,1,0:T(2,128)(2,1)S(1)} async-done(((bf16[4,2,640]{2,1,0:T(2,128)(2,1)}), bf16[4,2,640]{2,1,0:T(2,128)(2,1)S(1)}, u32[]{:S(2)}, u32[]{:S(2)}) %all-to-all-start.2) | async-done | bytes 10272 | tf_op jit(solution)/shard_map/all_to_all | solution.py:221
  26.7 4.3 %all-to-all-start.1 = ((bf16[160,32,128]{2,1,0:T(8,128)(2,1)}), bf16[160,32,128]{2,1,0:T(8,128)(2,1)}, u32[]{:S(2)}, u32[]{:S(2)}) async-start(bf16[160,32,128]{2,1,0:T(8,128)(2,1)} %param.10), calls=%async_computation.1 | async-start | bytes 2621440 | tf_op jit(solution)/shard_map/all_to_all | solution.py:220
  32.1 11.5 %collective-permute-done.1 = bf16[40,32,256]{2,1,0:T(8,128)(2,1)} collective-permute-done((bf16[40,32,256]{2,1,0:T(8,128)(2,1)}, bf16[40,32,256]{2,1,0:T(8,128)(2,1)}, u32[]{:S(2)}, u32[]{:S(2)}) %collective-permute-start.1) | collective-permute-done | bytes 655392 | tf_op jit(solution)/shard_map/ppermute | solution.py:165
  46.0 11.6 %collective-permute-done.3 = bf16[40,32,256]{2,1,0:T(8,128)(2,1)} collective-permute-done((bf16[40,32,256]{2,1,0:T(8,128)(2,1)}, bf16[40,32,256]{2,1,0:T(8,128)(2,1)}, u32[]{:S(2)}, u32[]{:S(2)}) %collective-permute-start.3) | collective-permute-done | bytes 655392 | tf_op jit(solution)/shard_map/ppermute | solution.py:165
  60.4 2.7 %gather_fusion.1 = bf16[160,32,256]{2,1,0:T(8,128)(2,1)S(1)} fusion(bf16[200,32,256]{2,1,0:T(8,128)(2,1)} %bitcast.150, s32[1024]{0:T(1024)S(1)} %pad_clamp_fusion), kind=kCustom, calls=%fused_computation.1 | custom fusion | bytes 5243520 | tf_op jit(solution)/shard_map/jit(_take)/gather | solution.py:214
  63.2 1.8 broadcast_select_fusion.1
  65.0 5.0 %all-to-all-start = ((bf16[160,32,256]{2,1,0:T(8,128)(2,1)}), bf16[160,32,256]{2,1,0:T(8,128)(2,1)S(1)}, u32[]{:S(2)}, u32[]{:S(2)}) async-start(bf16[160,32,256]{2,1,0:T(8,128)(2,1)} %broadcast_select_fusion.1), calls=%async_computation | async-start | bytes 5242880 | tf_op jit(solution)/shard_map/all_to_all | solution.py:219
  71.4 2.8 %copy.24 = bf16[4,40,32,128]{3,2,0,1:T(8,128)(2,1)} copy(bf16[4,40,32,128]{3,2,1,0:T(8,128)(2,1)} %bitcast.13) | data formatting | bytes 2621440 | tf_op jit(solution)/shard_map/all_to_all | solution.py:220
  74.2 54.3 %all-to-all-done = bf16[160,32,256]{2,1,0:T(8,128)(2,1)S(1)} async-done(((bf16[160,32,256]{2,1,0:T(8,128)(2,1)}), bf16[160,32,256]{2,1,0:T(8,128)(2,1)S(1)}, u32[]{:S(2)}, u32[]{:S(2)}) %all-to-all-start) | async-done | bytes 2621472 | tf_op jit(solution)/shard_map/all_to_all | solution.py:219
  130.7 5.5 %multiply_convert_fusion = (bf16[40,4,32,256]{3,2,0,1:T(8,128)(2,1)S(1)}, f32[40,4,32,256]{3,2,0,1:T(8,128)S(1)}) fusion(f32[40]{0:T(128)S(1)} %dynamic_slice.3, f32[4,32]{1,0:T(4,128)S(1)} %mul.53, f32[4,32,32,1]{1,0,2,3:T(4,128)S(1)} %bitcast.151, f32[40,4,32,256]{3,2,1,0:T(8,128)S(1)} %bitcast.144), kind=kOutput, calls=%fused_computation.9 | convolution fusion | flops 507248640 | bytes 13124256 | tf_op jit(solution)/shard_map/gce,fgck->fgek/dot_general | solution.py:173
  138.0 3.7 %fusion = f32[40,128,256]{2,1,0:T(8,128)} fusion(f32[40,4,32,256]{3,2,1,0:T(8,128)S(1)} %copy.29, f32[40]{0:T(128)S(1)} %dynamic_slice.3, f32[128]{0:T(128)S(1)} %sqrt.3), kind=kLoop, calls=%fused_computation.5 | loop fusion | flops 2621440 | bytes 10486432 | tf_op jit(solution)/shard_map/mul | solution.py:231
  141.7 7.7 %dot_general.26 = f32[2,128,128,40]{1,0,2,3:T(2,128)} reshape(f32[256,128,40]{0,1,2:T(8,128)} %bitcast.145) | data formatting | bytes 10485760 | tf_op jit(solution)/shard_map/fck,fc->k/dot_general | solution.py:234
  149.4 7.5 %multiply_reduce_fusion = f32[2,128]{1,0:T(2,128)S(1)} fusion(f32[2,128,128,40]{1,0,2,3:T(2,128)} %dot_general.26, f32[128,40]{0,1:T(8,128)S(1)} %copy.56), kind=kLoop, calls=%fused_computation.6 | loop fusion | flops 2621184 | bytes 5264384 | tf_op jit(solution)/shard_map/fck,fc->k/dot_general | solution.py:234
  157.8 15.6 %sum_all.1 = f32[448,128]{1,0:T(8,128)} custom-call(f32[448,128]{1,0:T(8,128)} %maximum_maximum_fusion.x_ref), custom_call_target="tpu_custom_call" | custom-call | tf_op jit(solution)/shard_map/sum_all/pallas_call | solution.py:113
  174.8 11.7 %cholesky.49 = f32[128,128]{1,0:T(8,128)S(1)} custom-call(f32[128,128]{1,0:T(8,128)S(1)} %cholesky.115), custom_call_target="Cholesky" | custom-call | tf_op jit(solution)/shard_map/jit(cholesky)/cholesky | solution.py:241
  186.6 9.8 %custom-call.18 = f32[1,128,128]{1,2,0:T(8,128)S(1)} custom-call(f32[1,128,128]{2,1,0:T(8,128)S(1)} %get-tuple-element.40), custom_call_target="InvertDiagBlocksLowerTriangular" | custom-call | tf_op jit(solution)/shard_map/jit(cholesky)/cholesky | solution.py:241
  196.9 11.7 %cholesky.103 = f32[128,128]{1,0:T(8,128)S(1)} custom-call(f32[128,128]{1,0:T(8,128)S(1)} %convolution_subtract_fusion.1), custom_call_target="Cholesky" | custom-call | tf_op jit(solution)/shard_map/jit(cholesky)/cholesky | solution.py:241
  211.1 4.2 %while.1 = (s32[]{:T(128)}, f32[256,256]{0,1:T(8,128)S(1)}, s32[2,2]{1,0:T(2,128)S(1)}, f32[2,128,128]{2,1,0:T(8,128)S(1)}, s32[]{:T(128)}) while((s32[]{:T(128)}, f32[256,256]{0,1:T(8,128)S(1)}, s32[2,2]{1,0:T(2,128)S(1)}, f32[2,128,128]{2,1,0:T(8,128)S(1)}, s32[]{:T(128)}) %tuple.30), condition=%wide.while_cond, body=%wide.while_body.sunk | while | flops 2 | bytes 393321 | solution.py:246
  215.2 19.9 %custom-call.19 = f32[2,128,128]{1,2,0:T(8,128)S(1)} custom-call(f32[2,128,128]{2,1,0:T(8,128)S(1)} %get-tuple-element.12), custom_call_target="InvertDiagBlocksLowerTriangular" | custom-call | tf_op jit(solution)/shard_map/triangular_solve | solution.py:246
  239.3 7.9 %apply_transform.1 = bf16[12288,256]{1,0:T(8,128)(2,1)} custom-call(bf16[12288,256]{1,0:T(8,128)(2,1)} %bitcast.146, bf16[256,256]{1,0:T(8,128)(2,1)} %fusion.17.w_ref), custom_call_target="tpu_custom_call" | custom-call | tf_op jit(solution)/shard_map/apply_transform/pallas_call | solution.py:149
  (104 shorter events, 27.3 us)
Async XLA Ops:
  8.7 6.7 %copy-start.4 = (f32[160,32]{0,1:T(8,128)S(1)}, f32[160,32]{0,1:T(8,128)}, u32[]{:S(2)}) copy-start(f32[160,32]{0,1:T(8,128)} %param.11) | copy-start | bytes 61444
  8.7 12.4 %copy-start.6 = (s32[160]{0:T(256)S(1)}, s32[160]{0:T(256)}, u32[]{:S(2)}) copy-start(s32[160]{0:T(256)} %param.16) | copy-start | bytes 1924
  10.3 20.7 %collective-permute-start = (bf16[40,32,256]{2,1,0:T(8,128)(2,1)}, bf16[40,32,256]{2,1,0:T(8,128)(2,1)}, u32[]{:S(2)}, u32[]{:S(2)}) collective-permute-start(bf16[40,32,256]{2,1,0:T(8,128)(2,1)} %get-tuple-element.34), channel_id=1, source_target_pairs={{0,24},{4,28},{8,0},{12,4},{16,8},{20,12},{24,16},{28,20},{1,25},{... | collective-permute-start | bytes 1966088 | tf_op jit(solution)/shard_map/ppermute | solution.py:165
  14.2 29.5 %collective-permute-start.1 = (bf16[40,32,256]{2,1,0:T(8,128)(2,1)}, bf16[40,32,256]{2,1,0:T(8,128)(2,1)}, u32[]{:S(2)}, u32[]{:S(2)}) collective-permute-start(bf16[40,32,256]{2,1,0:T(8,128)(2,1)} %get-tuple-element.33), channel_id=1, source_target_pairs={{0,28},{4,0},{8,4},{12,8},{16,12},{20,16},{24,20},{28,24},{1,29},{... | collective-permute-start | bytes 1966088 | tf_op jit(solution)/shard_map/ppermute | solution.py:165
  14.2 30.7 %collective-permute-start.2 = (bf16[40,32,256]{2,1,0:T(8,128)(2,1)}, bf16[40,32,256]{2,1,0:T(8,128)(2,1)}, u32[]{:S(2)}, u32[]{:S(2)}) collective-permute-start(bf16[40,32,256]{2,1,0:T(8,128)(2,1)} %get-tuple-element.32), channel_id=1, source_target_pairs={{0,4},{4,8},{8,12},{12,16},{16,20},{20,24},{24,28},{28,0},{1,5},{5... | collective-permute-start | bytes 1966088 | tf_op jit(solution)/shard_map/ppermute | solution.py:165
  14.7 42.9 %collective-permute-start.3 = (bf16[40,32,256]{2,1,0:T(8,128)(2,1)}, bf16[40,32,256]{2,1,0:T(8,128)(2,1)}, u32[]{:S(2)}, u32[]{:S(2)}) collective-permute-start(bf16[40,32,256]{2,1,0:T(8,128)(2,1)} %get-tuple-element.31), channel_id=1, source_target_pairs={{0,8},{4,12},{8,16},{12,20},{16,24},{20,28},{24,0},{28,4},{1,9},{5... | collective-permute-start | bytes 1966088 | tf_op jit(solution)/shard_map/ppermute | solution.py:165
  16.2 10.5 %all-to-all-start.2 = ((bf16[4,2,640]{2,1,0:T(2,128)(2,1)}), bf16[4,2,640]{2,1,0:T(2,128)(2,1)S(1)}, u32[]{:S(2)}, u32[]{:S(2)}) async-start(bf16[4,2,640]{2,1,0:T(2,128)(2,1)} %reshape.199), calls=%async_computation.2 | async-start | bytes 20480 | tf_op jit(solution)/shard_map/all_to_all | solution.py:221
  26.7 38.3 %all-to-all-start.1 = ((bf16[160,32,128]{2,1,0:T(8,128)(2,1)}), bf16[160,32,128]{2,1,0:T(8,128)(2,1)}, u32[]{:S(2)}, u32[]{:S(2)}) async-start(bf16[160,32,128]{2,1,0:T(8,128)(2,1)} %param.10), calls=%async_computation.1 | async-start | bytes 2621440 | tf_op jit(solution)/shard_map/all_to_all | solution.py:220
  58.7 1.7 copy-start.1
  65.0 5.7 %copy-start.7 = (f32[128]{0:T(128)S(1)}, f32[128]{0:T(128)}, u32[]{:S(2)}) copy-start(f32[128]{0:T(128)} %param.13) | copy-start | bytes 1540
  65.0 5.8 %copy-start.5 = (f32[128,32]{0,1:T(8,128)S(1)}, f32[128,32]{0,1:T(8,128)}, u32[]{:S(2)}) copy-start(f32[128,32]{0,1:T(8,128)} %param.12) | copy-start | bytes 49156
  65.0 63.6 %all-to-all-start = ((bf16[160,32,256]{2,1,0:T(8,128)(2,1)}), bf16[160,32,256]{2,1,0:T(8,128)(2,1)S(1)}, u32[]{:S(2)}, u32[]{:S(2)}) async-start(bf16[160,32,256]{2,1,0:T(8,128)(2,1)} %broadcast_select_fusion.1), calls=%async_computation | async-start | bytes 5242880 | tf_op jit(solution)/shard_map/all_to_all | solution.py:219
  128.6 1.3 copy-start
  137.1 0.9 copy-start.2
  149.4 7.6 %slice-start = ((f32[256,256]{1,0:T(8,128)}), f32[256,128]{1,0:T(8,128)S(1)}, s32[]{:S(2)}) async-start(f32[256,256]{1,0:T(8,128)} %copy-done.2), calls=%async_computation.3 | async-start | bytes 262144 | tf_op jit(solution)/shard_map/slice | solution.py:106
  174.6 63.1 %copy-start.3 = (f32[256,256]{1,0:T(8,128)S(1)}, f32[256,256]{1,0:T(8,128)}, u32[]{:S(2)}) copy-start(f32[256,256]{1,0:T(8,128)} %param.14) | copy-start | bytes 786436

commit v2 on v1

--- a/solution.py
+++ b/solution.py
@@ -159,6 +159,269 @@
     )(rows, transform)
 
 
+def exchange_kernel(
+    window, cap, chunks, share,
+    pick_ref, order_ref, slot_ref, live_ref, ens_ref, jac_ref, misfit_ref, high_ref, low_ref,
+    gram_ref, pull_ref,
+    ens_v, jac_s, jac_land, mis_land, mis_all, chosen, arr, col_s, col_land, white,
+    ens_sem, sems_t, sems_j, sems_m, sems_c,
+):
+    chans = lax.axis_size("chan")
+    tiles = lax.axis_size("tile")
+    tile = lax.axis_index("tile")
+    chan = lax.axis_index("chan")
+    reach = window // 2
+    level_part, members = ens_ref.shape[1], ens_ref.shape[2]
+    part, levels = jac_ref.shape[1], jac_ref.shape[2]
+    rows = chunks * share
+    load = pltpu.make_async_copy(ens_ref, ens_v, ens_sem)
+    load.start()
+
+    def chan_peer(step):
+        return lax.rem(chan + step, chans)
+
+    def tile_peer(slot):
+        return lax.rem(tile + slot - reach + tiles, tiles)
+
+    barrier = pltpu.get_barrier_semaphore()
+    for step in range(1, chans):
+        pl.semaphore_signal(barrier, inc=1, device_id={"chan": chan_peer(step)}, device_id_type=MESH)
+    for slot in range(window):
+        if slot != reach:
+            pl.semaphore_signal(barrier, inc=1, device_id={"tile": tile_peer(slot)}, device_id_type=MESH)
+
+    jac_copies, mis_copies = [], []
+    for step in range(1, chans):
+        peer = chan_peer(step)
+
+        def take_jac(i, carry, peer=peer):
+            jac_s[peer, i] = jac_ref[order_ref[peer * rows + i]]
+            return carry
+
+        lax.fori_loop(0, rows, take_jac, 0)
+        jac_copies.append(pltpu.make_async_remote_copy(
+            src_ref=jac_s.at[peer], dst_ref=jac_land.at[chan],
+            send_sem=sems_j.at[0, step], recv_sem=sems_j.at[1, step],
+            device_id={"chan": peer}, device_id_type=MESH))
+        mis_copies.append(pltpu.make_async_remote_copy(
+            src_ref=misfit_ref.at[peer], dst_ref=mis_land.at[chan],
+            send_sem=sems_m.at[0, step], recv_sem=sems_m.at[1, step],
+            device_id={"chan": peer}, device_id_type=MESH))
+
+    def own_jac(i, carry):
+        jac_land[chan, i] = jac_ref[order_ref[chan * rows + i]]
+        return carry
+
+    lax.fori_loop(0, rows, own_jac, 0)
+    mis_land[chan] = misfit_ref[chan]
+    pl.semaphore_wait(barrier, chans - 1 + window - 1)
+    for copy in mis_copies + jac_copies:
+        copy.start()
+
+    load.wait()
+    offsets = sorted((s for s in range(window) if s != reach), key=lambda s: abs(s - reach))
+    tile_copies = {}
+    waiting = None
+    for slot in offsets:
+        def take_col(i, carry, slot=slot):
+            chosen[slot, i] = ens_v[pick_ref[slot * cap + i]]
+            return carry
+
+        lax.fori_loop(0, cap, take_col, 0)
+        if waiting is not None:
+            waiting.start()
+        waiting = tile_copies[slot] = pltpu.make_async_remote_copy(
+            src_ref=chosen.at[slot], dst_ref=arr[slot],
+            send_sem=sems_t.at[0, slot], recv_sem=sems_t.at[1, slot],
+            device_id={"tile": tile_peer(slot)}, device_id_type=MESH)
+
+    def own_col(i, carry):
+        arr[reach][i] = ens_v[pick_ref[reach * cap + i]]
+        return carry
+
+    lax.fori_loop(0, cap, own_col, 0)
+    waiting.start()
+
+    landed = {reach}
+    col_copies = {}
+
+    def send_chunk(q):
+        for slot in (q, q + 1):
+            if slot not in landed:
+                tile_copies[slot].wait_recv()
+                landed.add(slot)
+
+        def pick(peer, i):
+            index = slot_ref[peer * rows + q * share + i] - q * cap
+            near = arr[q][jnp.clip(index, 0, cap - 1)]
+            far = arr[q + 1][jnp.clip(index - cap, 0, cap - 1)]
+            return lax.select(index < cap, near, far)
+
+        waiting = None
+        for step in range(1, chans):
+            peer = chan_peer(step)
+
+            def take(i, carry, peer=peer):
+                col_s[peer, q, i] = pick(peer, i)
+                return carry
+
+            lax.fori_loop(0, share, take, 0)
+            if waiting is not None:
+                waiting.start()
+            waiting = col_copies[q, step] = pltpu.make_async_remote_copy(
+                src_ref=col_s.at[peer, q], dst_ref=col_land.at[chan, q],
+                send_sem=sems_c.at[0, q, step], recv_sem=sems_c.at[1, q, step],
+                device_id={"chan": peer}, device_id_type=MESH)
+
+        def own(i, carry):
+            col_land[chan, q, i] = pick(chan, i)
+            return carry
+
+        lax.fori_loop(0, share, own, 0)
+        waiting.start()
+
+    sequence = sorted(range(chunks), key=lambda q: max(abs(q - reach), abs(q + 1 - reach)))
+    half = len(sequence) // 2
+    for q in sequence[:half]:
+        send_chunk(q)
+
+    for copy in mis_copies + jac_copies:
+        copy.wait_recv()
+    total = mis_land[0]
+    for z in range(1, chans):
+        total = total + mis_land[z]
+    mis_all[...] = total
+
+    def whiten(i, carry):
+        block = jac_land[:, i].reshape(chans * part, levels)
+        turned = jnp.dot(high_ref[...], block, preferred_element_type=jnp.float32)
+        turned = turned + jnp.dot(low_ref[...], block, preferred_element_type=jnp.float32)
+        turned = turned * live_ref[chan * rows + i]
+        first = turned.astype(jnp.bfloat16)
+        white[i, :, :levels] = first
+        white[i, :, levels:] = (turned - first.astype(jnp.float32)).astype(jnp.bfloat16)
+        return carry
+
+    lax.fori_loop(0, rows, whiten, 0)
+    for q in sequence[half:]:
+        send_chunk(q)
+
+    gram_ref[...] = jnp.zeros_like(gram_ref)
+    pull_ref[...] = jnp.zeros_like(pull_ref)
+    channels = chans * part
+    pair = 2 if share % 2 == 0 else 1
+
+    for q in sequence:
+        for step in range(1, chans):
+            col_copies[q, step].wait_recv()
+
+        def add(i, carry, q=q):
+            rounded, weights = [], []
+            for k in range(pair):
+                s = i * pair + k
+                block = col_land[:, q, s].reshape(levels, members)
+                both = jnp.concatenate([block, block], 0)
+                rounded.append(
+                    jnp.dot(white[q * share + s], both, preferred_element_type=jnp.float32).astype(jnp.bfloat16)
+                )
+                weights.append(mis_all[pl.ds(q * share + s, 1), :])
+            rounded = jnp.concatenate(rounded, 0)
+            weights = jnp.broadcast_to(jnp.concatenate(weights, 1), (8, pair * channels))
+            first = weights.astype(jnp.bfloat16).astype(jnp.float32)
+            line = lax.broadcasted_iota(jnp.int32, weights.shape, 0)
+            left = jnp.where(line == 0, first, jnp.where(line == 1, weights - first, 0.0))
+            pull_ref[...] += jnp.dot(left.astype(jnp.bfloat16), rounded, preferred_element_type=jnp.float32)
+            gram_ref[...] += lax.dot_general(
+                rounded, rounded, (((0,), (0,)), ((), ())), preferred_element_type=jnp.float32
+            )
+            return carry
+
+        lax.fori_loop(0, share // pair, add, 0)
+    for copy in mis_copies + jac_copies + list(tile_copies.values()) + list(col_copies.values()):
+        copy.wait_send()
+
+
+def fits(ensemble, jacobian, column_pick, footprint_slot):
+    chans = lax.axis_size("chan")
+    window, cap = column_pick.shape[1:]
+    return (
+        footprint_slot.shape[0] == (window - 1) * cap
+        and cap % chans == 0
+        and window <= lax.axis_size("tile")
+        and ensemble.shape[1] % 16 == 0
+        and jacobian.shape[1] % 16 == 0
+        and ensemble.shape[1] * chans == jacobian.shape[2]
+        and jacobian.shape[1] * chans == jacobian.shape[2]
+        and jacobian.shape[2] % 128 == 0
+    )
+
+
+def exchange(ensemble, jacobian, innovation, error_vectors, error_values, column_pick, footprint_slot, footprint_count):
+    chans = lax.axis_size("chan")
+    chan = lax.axis_index("chan")
+    window, cap = column_pick.shape[1:]
+    foot_rows = footprint_slot.shape[0]
+    chunks = window - 1
+    share = cap // chans
+    rows = chunks * share
+    part, levels = jacobian.shape[1:]
+    level_part, members = ensemble.shape[1:]
+    channels = part * chans
+    group = error_vectors.shape[1]
+    rank = jnp.sum(footprint_slot[None, :] < footprint_slot[:, None], axis=1, dtype=jnp.int32)
+    place = jnp.arange(foot_rows, dtype=jnp.int32)
+    spot = place % rows
+    wanted = (spot // share) * cap + (place // rows) * share + spot % share
+    match = rank[None, :] == wanted[:, None]
+    order = jnp.sum(jnp.where(match, place[None, :], 0), axis=1)
+    slots = jnp.sum(jnp.where(match, footprint_slot[None, :], 0), axis=1)
+    live = (order < footprint_count[0]).astype(jnp.float32)
+    spread = jnp.tile(error_vectors, (1, channels // group))
+    group_of = jnp.arange(channels) // group
+    basis = jnp.where(group_of[:, None] == group_of[None, :], spread, 0.0) / jnp.sqrt(error_values)[None, :]
+    turned = basis.T
+    high = turned.astype(jnp.bfloat16)
+    low = (turned - high.astype(jnp.float32)).astype(jnp.bfloat16)
+    ours = lax.dynamic_slice_in_dim(basis, chan * part, part, 0)
+    misfit = jnp.dot(innovation, ours, precision=lax.Precision.HIGHEST)
+    misfit = jnp.dot(match.astype(jnp.float32), misfit, precision=lax.Precision.HIGHEST)
+    misfit = misfit.reshape(chans, rows, channels)
+    vmem = pl.BlockSpec(memory_space=pltpu.VMEM)
+    smem = pl.BlockSpec(memory_space=pltpu.SMEM)
+    half = jnp.bfloat16
+    gram, pull = pl.pallas_call(
+        functools.partial(exchange_kernel, window, cap, chunks, share),
+        out_shape=(
+            jax.ShapeDtypeStruct((members, members), jnp.float32),
+            jax.ShapeDtypeStruct((8, members), jnp.float32),
+        ),
+        in_specs=[smem] * 4 + [pl.BlockSpec(memory_space=pl.ANY)] + [vmem] * 4,
+        out_specs=(vmem, vmem),
+        scratch_shapes=[
+            pltpu.VMEM(ensemble.shape, half),
+            pltpu.VMEM((chans, rows, part, levels), half),
+            pltpu.VMEM((chans, rows, part, levels), half),
+            pltpu.VMEM((chans, rows, channels), jnp.float32),
+            pltpu.VMEM((rows, channels), jnp.float32),
+            pltpu.VMEM((window, cap, level_part, members), half),
+            [pltpu.VMEM((cap, level_part, members), half) for _ in range(window)],
+            pltpu.VMEM((chans, chunks, share, level_part, members), half),
+            pltpu.VMEM((chans, chunks, share, level_part, members), half),
+            pltpu.VMEM((rows, channels, 2 * levels), half),
+            pltpu.SemaphoreType.DMA,
+            pltpu.SemaphoreType.DMA((2, window)),
+            pltpu.SemaphoreType.DMA((2, chans)),
+            pltpu.SemaphoreType.DMA((2, chans)),
+            pltpu.SemaphoreType.DMA((2, chunks, chans)),
+        ],
+        compiler_params=pltpu.CompilerParams(
+            collective_id=1, has_side_effects=True, vmem_limit_bytes=48 * 1024 * 1024
+        ),
+        name="exchange",
+    )(column_pick.reshape(-1), order, slots, live, ensemble, jacobian, misfit, high, low)
+    return gram, pull[0] + pull[1]
+
+
 def from_behind(value, axis, steps):
     count = lax.axis_size(axis)
     pairs = [(source, (source + steps) % count) for source in range(count)]
@@ -183,16 +446,8 @@
     return turned.reshape(row_count, channels)
 
 
-def local(
-    ensemble,
-    jacobian,
-    innovation,
-    error_vectors,
-    error_values,
-    ensemble_vectors,
-    column_pick,
-    footprint_slot,
-    footprint_count,
+def exchange_plain(
+    ensemble, jacobian, innovation, error_vectors, error_values, column_pick, footprint_slot, footprint_count
 ):
     window = column_pick.shape[1]
     capacity = column_pick.shape[2]
@@ -236,6 +491,25 @@
     gram_sum = lax.dot_general(
         rounded, rounded, (((0,), (0,)), ((), ())), preferred_element_type=jnp.float32
     )
+    return gram_sum, pull_sum
+
+
+def local(
+    ensemble,
+    jacobian,
+    innovation,
+    error_vectors,
+    error_values,
+    ensemble_vectors,
+    column_pick,
+    footprint_slot,
+    footprint_count,
+):
+    members = ensemble.shape[2]
+    route = exchange if fits(ensemble, jacobian, column_pick, footprint_slot) else exchange_plain
+    gram_sum, pull_sum = route(
+        ensemble, jacobian, innovation, error_vectors, error_values, column_pick, footprint_slot, footprint_count
+    )
     gram_sum, pull_sum = sum_all(gram_sum, pull_sum)
     system = gram_sum + (members - 1) * jnp.eye(members, dtype=jnp.float32)
     factor = jnp.linalg.cholesky(system)

time: 248 us -> 195 us (0.79)
  Pallas kernels: 23.6 us -> 121 us
  waiting for transfers between devices: 83 us -> 0 us
  local copies, waits for them, and re-layouts: 36 us -> 8.98 us
  starting transfers between devices: 19.3 us -> 0 us
  other arithmetic: 71.9 us -> 58.2 us
  matrix products: 11.1 us -> 4.35 us
    pallas_call x0 -> x1, Pallas kernels: none -> 94.2 us  [exchange(): pl.pallas_call(functools.partial(exchange_kernel, window, cap, chunks, sh...]
    all_to_all x3 -> x0, waiting for transfers between devices: 59.9 us -> none  [the longest x1 54.3 us: local(): lax.all_to_all(columns, 'chan', split_axis=0, concat_axis=1, tiled=True)]
    ppermute x4 -> x0, waiting for transfers between devices: 23.1 us -> none  [from_behind(): return lax.ppermute(value, axis, pairs)]
    all_to_all x3 -> x0, starting transfers between devices: 14.2 us -> none  [the longest x1 5 us: local(): lax.all_to_all(columns, 'chan', split_axis=0, concat_axis=1, tiled=True)]
    gather x2 -> x0, local copies, waits for them, and re-layouts: 8.23 us -> none  [the longest x1 5.49 us: local(): jnp.take(ensemble, column_pick[0].reshape(-1), axis=0)]
    dot_general x1 -> x0, local copies, waits for them, and re-layouts: 7.71 us -> none  [local(): jnp.einsum('fck,fc->k', whitened, misfit, precision=lax.Precision.HIGHEST)]
    dot_general x1 -> x0, other arithmetic: 7.54 us -> none  [local(): jnp.einsum('fck,fc->k', whitened, misfit, precision=lax.Precision.HIGHEST)]
    dot_general x4 -> x2, matrix products: 7.33 us -> 0.6 us  [the longest x1 0.33 us: exchange(): misfit = jnp.dot(innovation, ours, precision=lax.Precision.HIGHEST)]
  transfers between devices with their start and end apart: 7 -> 0, of which waited for: 4 -> 0; matrix products, arithmetic and copies ran while one was open for 5% -> 0% of each run, Pallas kernels for 0% -> 0%
where the time goes in v2:
time: 195 us; the launch traced here: 194 us
  Pallas kernels  121 us (62%)
  other arithmetic  58.2 us (30%)
  local copies, waits for them, and re-layouts  8.98 us (5%)
  matrix products  4.35 us (2%)
  between operations  2.26 us (1%)
    pallas_call x1, Pallas kernels, exchange(): pl.pallas_call(functools.partial(exchange_kernel, window, cap, chunks, sh...  94.2 us
    another operation x6, other arithmetic, local(): factor = jnp.linalg.cholesky(system)  34 us
    another operation x3, other arithmetic, local(): lax.linalg.triangular_solve(factor, ensemble_vectors, left_side=True, low...  19.9 us
    pallas_call x1, Pallas kernels, sum_all(): pl.pallas_call(functools.partial(sum_kernel, piece), out_shape=jax.ShapeD...  18.4 us
    pallas_call x1, Pallas kernels, apply_transform(): pl.pallas_call(apply_kernel, grid=(count // block,), out_shape=jax.ShapeD...  7.92 us
    another operation x10, local copies, waits for them, and re-layouts  4.12 us

profile of v2, /device:TPU:0, one launch (start us, length us, event | category | flops | bytes accessed | tf_op | source)
XLA Modules:
  0.0 194.4 jit_solution(11252861758977477720)
XLA Ops:
  0.7 0.7 sqrt.3
  1.4 0.9 convert_reduce_fusion
  2.5 0.9 fusion.10
  3.4 0.7 reduce.12
  4.2 0.7 tile.4
  6.0 1.3 copy-done.1
  7.3 94.2 %exchange.1 = (f32[256,256]{1,0:T(8,128)S(1)}, f32[8,256]{1,0:T(8,128)S(1)}) custom-call(s32[200]{0:T(256)S(1)} %reshape.134.pick_ref, s32[160]{0:T(256)S(1)} %get-tuple-element.30.order_ref, s32[160]{0:T(256)S(1)} %get-tuple-element.29.slot_ref, f32[160]{0:T(256)S(1)} %compare_convert_fusion.live_ref, bf16[384,32,256]{2,1,0:T(8,128)(2,1)} %ens_ref.1, ...), custom_call_target="tpu_custom_call" | custom-call | tf_op jit(solution)/shard_map/exchange/pallas_call | solution.py:392
  101.5 0.8 maximum_maximum_fusion.x_ref
  102.3 18.4 %sum_all.1 = f32[448,128]{1,0:T(8,128)} custom-call(f32[448,128]{1,0:T(8,128)} %maximum_maximum_fusion.x_ref), custom_call_target="tpu_custom_call" | custom-call | tf_op jit(solution)/shard_map/sum_all/pallas_call | solution.py:113
  120.8 0.9 fusion.36
  122.2 11.7 %cholesky.50 = f32[128,128]{1,0:T(8,128)S(1)} custom-call(f32[128,128]{1,0:T(8,128)S(1)} %cholesky.115), custom_call_target="Cholesky" | custom-call | tf_op jit(solution)/shard_map/jit(cholesky)/cholesky | solution.py:515
  134.0 9.8 %custom-call.18 = f32[1,128,128]{1,2,0:T(8,128)S(1)} custom-call(f32[1,128,128]{2,1,0:T(8,128)S(1)} %get-tuple-element.49), custom_call_target="InvertDiagBlocksLowerTriangular" | custom-call | tf_op jit(solution)/shard_map/jit(cholesky)/cholesky | solution.py:515
  144.3 11.7 %cholesky.103 = f32[128,128]{1,0:T(8,128)S(1)} custom-call(f32[128,128]{1,0:T(8,128)S(1)} %convolution_subtract_fusion.1), custom_call_target="Cholesky" | custom-call | tf_op jit(solution)/shard_map/jit(cholesky)/cholesky | solution.py:515
  156.3 0.7 compare_reduce_fusion
  158.3 4.2 %while.1 = (s32[]{:T(128)}, f32[256,256]{0,1:T(8,128)S(1)}, s32[2,2]{1,0:T(2,128)S(1)}, f32[2,128,128]{2,1,0:T(8,128)S(1)}, s32[]{:T(128)}) while((s32[]{:T(128)}, f32[256,256]{0,1:T(8,128)S(1)}, s32[2,2]{1,0:T(2,128)S(1)}, f32[2,128,128]{2,1,0:T(8,128)S(1)}, s32[]{:T(128)}) %tuple.30), condition=%wide.while_cond, body=%wide.while_body.sunk | while | flops 2 | bytes 393329 | solution.py:520
  158.3 0.6 fusion.48
  158.9 1.4 dynamic-slice.7
  160.4 0.6 fusion.48
  161.0 1.4 dynamic-slice.7
  162.5 19.9 %custom-call.19 = f32[2,128,128]{1,2,0:T(8,128)S(1)} custom-call(f32[2,128,128]{2,1,0:T(8,128)S(1)} %get-tuple-element.16), custom_call_target="InvertDiagBlocksLowerTriangular" | custom-call | tf_op jit(solution)/shard_map/triangular_solve | solution.py:520
  182.4 0.8 fusion.19
  183.3 0.8 fusion.3
  185.8 0.7 fusion.5.w_ref
  186.5 7.9 %apply_transform.1 = bf16[12288,256]{1,0:T(8,128)(2,1)} custom-call(bf16[12288,256]{1,0:T(8,128)(2,1)} %bitcast.93, bf16[256,256]{1,0:T(8,128)(2,1)} %fusion.5.w_ref), custom_call_target="tpu_custom_call" | custom-call | tf_op jit(solution)/shard_map/apply_transform/pallas_call | solution.py:149
  (55 shorter events, 4.5 us)
Async XLA Ops:
  0.0 5.3 %copy-start = (f32[160,32]{0,1:T(8,128)S(1)}, f32[160,32]{0,1:T(8,128)}, u32[]{:S(2)}) copy-start(f32[160,32]{0,1:T(8,128)} %param.11) | copy-start | bytes 61444
  5.9 1.3 copy-start.1
  101.5 83.5 %copy-start.2 = (f32[256,256]{1,0:T(8,128)S(1)}, f32[256,256]{1,0:T(8,128)}, u32[]{:S(2)}) copy-start(f32[256,256]{1,0:T(8,128)} %param.14) | copy-start | bytes 786436

commit v3 on v2

--- a/solution.py
+++ b/solution.py
@@ -110,7 +110,7 @@
         ],
         0,
     )
-    out = pl.pallas_call(
+    return pl.pallas_call(
         functools.partial(sum_kernel, piece),
         out_shape=jax.ShapeDtypeStruct(flat.shape, jnp.float32),
         in_specs=[pl.BlockSpec(memory_space=pltpu.VMEM)],
@@ -128,35 +128,109 @@
         compiler_params=pltpu.CompilerParams(collective_id=0, has_side_effects=True),
         name="sum_all",
     )(flat)
-    top = out[:half]
-    across = out[half : 2 * half]
-    low = out[2 * half : 3 * half]
-    gram = jnp.concatenate(
-        [jnp.concatenate([top, across], 1), jnp.concatenate([across.T, low], 1)], 0
-    )
-    return gram, out[3 * half : 3 * half + 2].reshape(members)
-
-
-def apply_kernel(x_ref, w_ref, o_ref):
-    o_ref[...] = jnp.dot(x_ref[...], w_ref[...], preferred_element_type=jnp.float32).astype(o_ref.dtype)
-
-
-def apply_transform(rows, transform):
-    count, members = rows.shape
-    block = min(count, 2048)
-    while count % block:
-        block //= 2
+
+
+def invert_factor(d_ref, y_ref):
+    size = d_ref.shape[0]
+    step = 8
+    shape = d_ref.shape
+    y_ref[...] = (
+        lax.broadcasted_iota(jnp.int32, shape, 0) == lax.broadcasted_iota(jnp.int32, shape, 1)
+    ).astype(jnp.float32)
+    for start in range(0, size, step):
+        below = d_ref[start:, :]
+        right = y_ref[start:, :]
+        line = lax.broadcasted_iota(jnp.int32, below.shape, 0)
+        columns = [
+            jnp.broadcast_to(below[:, start + j : start + j + 1], below.shape) for j in range(step)
+        ]
+        rows = [below[j : j + 1, :] for j in range(step)]
+        others = [right[j : j + 1, :] for j in range(step)]
+        for j in range(step):
+            pivot = columns[j][j : j + 1, :]
+            inverse = 1.0 / pivot
+            under = jnp.where(line > j, columns[j], 0.0)
+            row = rows[j] * inverse
+            other = others[j] * inverse
+            for k in range(j + 1, step):
+                entry = columns[j][k : k + 1, :]
+                columns[k] = columns[k] - under * (columns[k][j : j + 1, :] * inverse)
+                rows[k] = rows[k] - entry * row
+                others[k] = others[k] - entry * other
+            below = below - under * row
+            right = right - under * other
+            y_ref[start + j : start + j + 1, :] = others[j] * (1.0 / jnp.sqrt(pivot))
+        if start + step < size:
+            d_ref[start + step :, :] = below[step:, :]
+            y_ref[start + step :, :] = right[step:, :]
+
+
+def finish_kernel(pieces, sum_ref, vec_ref, ens_ref, out_ref, d_ref, first, second, ens_v, out_v, load_sem, sems):
+    half = d_ref.shape[0]
+    members = 2 * half
+    load = pltpu.make_async_copy(ens_ref, ens_v, load_sem)
+    load.start()
+    dims = lambda a, b: (((a,), (b,)), ((), ()))
+
+    def dot(x, y, a=1, b=0):
+        return lax.dot_general(
+            x, y, dims(a, b), precision=lax.Precision.HIGHEST, preferred_element_type=jnp.float32
+        )
+
+    eye = (
+        lax.broadcasted_iota(jnp.int32, (half, half), 0) == lax.broadcasted_iota(jnp.int32, (half, half), 1)
+    ).astype(jnp.float32) * (members - 1)
+    d_ref[...] = sum_ref[:half, :] + eye
+    invert_factor(d_ref, first)
+    across = dot(first[...], sum_ref[half : 2 * half, :])
+    d_ref[...] = sum_ref[2 * half : 3 * half, :] + eye - dot(across, across, 0, 0)
+    invert_factor(d_ref, second)
+    low = -dot(second[...], dot(across, first[...], 0, 0))
+    pull = sum_ref[3 * half : 3 * half + 8, :]
+    top_half = jnp.sum(first[...] * pull[0:1, :], axis=1, keepdims=True)
+    low_half = jnp.sum(low * pull[0:1, :] + second[...] * pull[1:2, :], axis=1, keepdims=True)
+    scale = float(members - 1) ** 0.5
+    top_right = scale * vec_ref[:half, :] + top_half
+    low_right = scale * vec_ref[half:, :] + low_half
+    transform = jnp.concatenate(
+        [dot(first[...], top_right, 0, 0) + dot(low, low_right, 0, 0), dot(second[...], low_right, 0, 0)], 0
+    ).astype(jnp.bfloat16)
+    load.wait()
+    size = ens_ref.shape[0] // pieces
+    writes = []
+    for i in range(pieces):
+        span = pl.ds(i * size, size)
+        out_v[span, :] = jnp.dot(
+            ens_v[span, :], transform, preferred_element_type=jnp.float32
+        ).astype(jnp.bfloat16)
+        writes.append(pltpu.make_async_copy(out_v.at[span], out_ref.at[span], sems.at[i]))
+        writes[-1].start()
+    for write in writes:
+        write.wait()
+
+
+def finish(sums, ensemble_vectors, rows):
+    members = ensemble_vectors.shape[0]
+    half = members // 2
+    pieces = 8
+    vmem = pl.BlockSpec(memory_space=pltpu.VMEM)
     return pl.pallas_call(
-        apply_kernel,
-        grid=(count // block,),
+        functools.partial(finish_kernel, pieces),
         out_shape=jax.ShapeDtypeStruct(rows.shape, rows.dtype),
-        in_specs=[
-            pl.BlockSpec((block, members), lambda i: (i, 0)),
-            pl.BlockSpec((members, members), lambda i: (0, 0)),
+        in_specs=[vmem, vmem, pl.BlockSpec(memory_space=pl.ANY)],
+        out_specs=pl.BlockSpec(memory_space=pl.ANY),
+        scratch_shapes=[
+            pltpu.VMEM((half, half), jnp.float32),
+            pltpu.VMEM((half, half), jnp.float32),
+            pltpu.VMEM((half, half), jnp.float32),
+            pltpu.VMEM(rows.shape, rows.dtype),
+            pltpu.VMEM(rows.shape, rows.dtype),
+            pltpu.SemaphoreType.DMA,
+            pltpu.SemaphoreType.DMA((pieces,)),
         ],
-        out_specs=pl.BlockSpec((block, members), lambda i: (i, 0)),
-        name="apply_transform",
-    )(rows, transform)
+        compiler_params=pltpu.CompilerParams(vmem_limit_bytes=40 * 1024 * 1024),
+        name="finish",
+    )(sums, ensemble_vectors, rows)
 
 
 def exchange_kernel(
@@ -510,19 +584,8 @@
     gram_sum, pull_sum = route(
         ensemble, jacobian, innovation, error_vectors, error_values, column_pick, footprint_slot, footprint_count
     )
-    gram_sum, pull_sum = sum_all(gram_sum, pull_sum)
-    system = gram_sum + (members - 1) * jnp.eye(members, dtype=jnp.float32)
-    factor = jnp.linalg.cholesky(system)
-    halfway = lax.linalg.triangular_solve(factor, pull_sum[:, None], left_side=True, lower=True)
-    mean_weights = lax.linalg.triangular_solve(
-        factor, halfway, left_side=True, lower=True, transpose_a=True
-    )[:, 0]
-    spread = jnp.sqrt(members - 1.0) * lax.linalg.triangular_solve(
-        factor, ensemble_vectors, left_side=True, lower=True, transpose_a=True
-    )
-    transform = (spread + mean_weights[:, None]).astype(jnp.bfloat16)
-    flat_rows = ensemble.reshape(-1, members)
-    updated = apply_transform(flat_rows, transform)
+    sums = sum_all(gram_sum, pull_sum)
+    updated = finish(sums, ensemble_vectors, ensemble.reshape(-1, members))
     return updated.reshape(ensemble.shape)
 
 

time: 195 us -> 137 us (0.70)
  other arithmetic: 58.2 us -> 5.04 us
  matrix products: 4.35 us -> 0.59 us
  local copies, waits for them, and re-layouts: 8.98 us -> 5.87 us
  Pallas kernels: 121 us -> 124 us
    another operation x10 -> x0, other arithmetic: 53.9 us -> none  [the longest x6 34 us: local(): factor = jnp.linalg.cholesky(system)]
    another operation x20 -> x0, local copies, waits for them, and re-layouts: 5.32 us -> none
    pallas_call x1, Pallas kernels: 7.92 us -> 11.7 us  [finish(): pl.pallas_call(functools.partial(finish_kernel, pieces), out_shape=jax.Sh...]
    another operation x11 -> x0, matrix products: 3.74 us -> none  [the longest x3 1.84 us: local(): lax.linalg.triangular_solve(factor, pull_sum[:, None], left_side=True, lo...]
    unnamed x7 -> x10, local copies, waits for them, and re-layouts: 1.45 us -> 5.04 us
where the time goes in v3:
time: 137 us; the launch traced here: 136 us
  Pallas kernels  124 us (91%)
  local copies, waits for them, and re-layouts  5.87 us (4%)
  other arithmetic  5.04 us (4%)
    pallas_call x1, Pallas kernels, exchange(): pl.pallas_call(functools.partial(exchange_kernel, window, cap, chunks, sh...  94 us
    pallas_call x1, Pallas kernels, sum_all(): pl.pallas_call(functools.partial(sum_kernel, piece), out_shape=jax.ShapeD...  18.4 us
    pallas_call x1, Pallas kernels, finish(): pl.pallas_call(functools.partial(finish_kernel, pieces), out_shape=jax.Sh...  11.7 us
    unnamed x10, local copies, waits for them, and re-layouts  5.04 us

profile of v3, /device:TPU:0, one launch (start us, length us, event | category | flops | bytes accessed | tf_op | source)
XLA Modules:
  0.0 136.5 jit_solution(15991473571705035893)
XLA Ops:
  0.0 0.0 copy-start
  0.0 0.0 copy-start.4
  0.7 0.7 sqrt.3
  1.4 0.9 convert_reduce_fusion
  2.4 0.1 pad.3.clone
  2.4 0.9 fusion.3
  3.3 0.7 reduce
  4.0 0.1 reshape.83.pick_ref
  4.1 0.8 fusion.7
  4.9 0.8 fusion.6
  5.8 0.0 copy-done
  5.8 0.3 fusion.8
  6.1 0.3 fusion
  6.4 0.0 copy-start.2
  6.4 1.3 copy-done.2
  7.7 94.0 %exchange.1 = (f32[256,256]{1,0:T(8,128)S(1)}, f32[8,256]{1,0:T(8,128)S(1)}) custom-call(s32[200]{0:T(256)S(1)} %reshape.83.pick_ref, s32[160]{0:T(256)S(1)} %get-tuple-element.10.order_ref, s32[160]{0:T(256)S(1)} %get-tuple-element.9.slot_ref, f32[160]{0:T(256)S(1)} %compare_convert_fusion.live_ref, bf16[384,32,256]{2,1,0:T(8,128)(2,1)} %ens_ref.1, ...), custom_call_target="tpu_custom_call" | custom-call | tf_op jit(solution)/shard_map/exchange/pallas_call | solution.py:466
  101.8 0.8 maximum_maximum_fusion.x_ref
  102.6 18.4 %sum_all.1.sum_ref = f32[448,128]{1,0:T(8,128)} custom-call(f32[448,128]{1,0:T(8,128)} %maximum_maximum_fusion.x_ref), custom_call_target="tpu_custom_call" | custom-call | tf_op jit(solution)/shard_map/sum_all/pallas_call | solution.py:113
  121.0 0.0 copy-done.4
  121.0 0.0 copy-start.1
  121.0 2.8 %copy-done.1 = bf16[384,32,256]{2,1,0:T(8,128)(2,1)S(1)} copy-done((bf16[384,32,256]{2,1,0:T(8,128)(2,1)S(1)}, bf16[384,32,256]{2,1,0:T(8,128)(2,1)}, u32[]{:S(2)}) %copy-start.1) | copy-done | bytes 6291480
  123.8 0.0 copy-start.3
  123.8 0.9 copy-done.3
  124.8 11.7 %finish.1 = bf16[12288,256]{1,0:T(8,128)(2,1)} custom-call(f32[448,128]{1,0:T(8,128)S(1)} %copy-done.3, f32[256,256]{1,0:T(8,128)S(1)} %copy-done.4, bf16[12288,256]{1,0:T(8,128)(2,1)S(1)} %bitcast.23), custom_call_target="tpu_custom_call" | custom-call | tf_op jit(solution)/shard_map/finish/pallas_call | solution.py:217
  (7 shorter events, 0.1 us)
Async XLA Ops:
  0.0 5.8 %copy-start = (f32[160,32]{0,1:T(8,128)S(1)}, f32[160,32]{0,1:T(8,128)}, u32[]{:S(2)}) copy-start(f32[160,32]{0,1:T(8,128)} %param.11) | copy-start | bytes 61444
  0.0 121.0 %copy-start.4 = (f32[256,256]{1,0:T(8,128)S(1)}, f32[256,256]{1,0:T(8,128)}, u32[]{:S(2)}) copy-start(f32[256,256]{1,0:T(8,128)} %vec_ref.1) | copy-start | bytes 786436
  6.4 1.3 copy-start.2
  121.0 2.8 %copy-start.1 = (bf16[384,32,256]{2,1,0:T(8,128)(2,1)S(1)}, bf16[384,32,256]{2,1,0:T(8,128)(2,1)}, u32[]{:S(2)}) copy-start(bf16[384,32,256]{2,1,0:T(8,128)(2,1)} %ens_ref.1) | copy-start | bytes 18874372
  123.8 0.9 copy-start.3

commit v4 on v3

--- a/solution.py
+++ b/solution.py
@@ -28,7 +28,6 @@
     chans = lax.axis_size("chan")
     tile = lax.axis_index("tile")
     chan = lax.axis_index("chan")
-    greet(("tile", "chan"))
 
     def rows_of(index):
         return pl.ds(pl.multiple_of(index * piece, 8), piece)
@@ -93,13 +92,34 @@
         copy.wait_send()
 
 
+def sum_kernel_alone(piece, *refs):
+    greet(("tile", "chan"))
+    sum_kernel(piece, *refs)
+
+
+def sum_scratch(tiles, chans, piece, half):
+    return [
+        pltpu.VMEM((tiles, piece, half), jnp.float32),
+        pltpu.VMEM((chans, piece, half), jnp.float32),
+        pltpu.VMEM((piece, half), jnp.float32),
+        pltpu.VMEM((piece, half), jnp.float32),
+        pltpu.VMEM((tiles, piece, half), jnp.float32),
+        pltpu.SemaphoreType.DMA((2, tiles)),
+        pltpu.SemaphoreType.DMA((2, chans)),
+        pltpu.SemaphoreType.DMA((2, tiles)),
+    ]
+
+
+def piece_rows(tiles, half):
+    return -(-(3 * half + 8) // (8 * tiles)) * 8
+
+
 def sum_all(gram, pull):
     tiles = lax.axis_size("tile")
     chans = lax.axis_size("chan")
     members = gram.shape[0]
     half = members // 2
-    used = 3 * half + 8
-    piece = -(-used // (8 * tiles)) * 8
+    piece = piece_rows(tiles, half)
     flat = jnp.concatenate(
         [
             gram[:half, :half],
@@ -111,20 +131,11 @@
         0,
     )
     return pl.pallas_call(
-        functools.partial(sum_kernel, piece),
+        functools.partial(sum_kernel_alone, piece),
         out_shape=jax.ShapeDtypeStruct(flat.shape, jnp.float32),
         in_specs=[pl.BlockSpec(memory_space=pltpu.VMEM)],
         out_specs=pl.BlockSpec(memory_space=pltpu.VMEM),
-        scratch_shapes=[
-            pltpu.VMEM((tiles, piece, half), jnp.float32),
-            pltpu.VMEM((chans, piece, half), jnp.float32),
-            pltpu.VMEM((piece, half), jnp.float32),
-            pltpu.VMEM((piece, half), jnp.float32),
-            pltpu.VMEM((tiles, piece, half), jnp.float32),
-            pltpu.SemaphoreType.DMA((2, tiles)),
-            pltpu.SemaphoreType.DMA((2, chans)),
-            pltpu.SemaphoreType.DMA((2, tiles)),
-        ],
+        scratch_shapes=sum_scratch(tiles, chans, piece, half),
         compiler_params=pltpu.CompilerParams(collective_id=0, has_side_effects=True),
         name="sum_all",
     )(flat)
@@ -217,8 +228,8 @@
     return pl.pallas_call(
         functools.partial(finish_kernel, pieces),
         out_shape=jax.ShapeDtypeStruct(rows.shape, rows.dtype),
-        in_specs=[vmem, vmem, pl.BlockSpec(memory_space=pl.ANY)],
-        out_specs=pl.BlockSpec(memory_space=pl.ANY),
+        in_specs=[vmem, vmem, pl.BlockSpec(memory_space=pltpu.HBM)],
+        out_specs=pl.BlockSpec(memory_space=pltpu.HBM),
         scratch_shapes=[
             pltpu.VMEM((half, half), jnp.float32),
             pltpu.VMEM((half, half), jnp.float32),
@@ -234,11 +245,12 @@
 
 
 def exchange_kernel(
-    window, cap, chunks, share,
-    pick_ref, order_ref, slot_ref, live_ref, ens_ref, jac_ref, misfit_ref, high_ref, low_ref,
-    gram_ref, pull_ref,
+    window, cap, chunks, share, piece,
+    pick_ref, order_ref, slot_ref, live_ref, ens_ref, jac_ref, innov_ref, vec_ref, val_ref,
+    sums_ref,
+    gram_ref, pull_ref, parts_ref, basis_ref, high_ref, low_ref, innov_v, misfit_ref,
     ens_v, jac_s, jac_land, mis_land, mis_all, chosen, arr, col_s, col_land, white,
-    ens_sem, sems_t, sems_j, sems_m, sems_c,
+    ens_sem, sems_t, sems_j, sems_m, sems_c, *sum_refs,
 ):
     chans = lax.axis_size("chan")
     tiles = lax.axis_size("tile")
@@ -260,9 +272,10 @@
     barrier = pltpu.get_barrier_semaphore()
     for step in range(1, chans):
         pl.semaphore_signal(barrier, inc=1, device_id={"chan": chan_peer(step)}, device_id_type=MESH)
-    for slot in range(window):
-        if slot != reach:
-            pl.semaphore_signal(barrier, inc=1, device_id={"tile": tile_peer(slot)}, device_id_type=MESH)
+    for step in range(1, tiles):
+        pl.semaphore_signal(
+            barrier, inc=1, device_id={"tile": lax.rem(tile + step, tiles)}, device_id_type=MESH
+        )
 
     jac_copies, mis_copies = [], []
     for step in range(1, chans):
@@ -287,9 +300,8 @@
         return carry
 
     lax.fori_loop(0, rows, own_jac, 0)
-    mis_land[chan] = misfit_ref[chan]
-    pl.semaphore_wait(barrier, chans - 1 + window - 1)
-    for copy in mis_copies + jac_copies:
+    pl.semaphore_wait(barrier, chans - 1 + tiles - 1)
+    for copy in jac_copies:
         copy.start()
 
     load.wait()
@@ -298,7 +310,7 @@
     waiting = None
     for slot in offsets:
         def take_col(i, carry, slot=slot):
-            chosen[slot, i] = ens_v[pick_ref[slot * cap + i]]
+            chosen[slot, i] = ens_v[pick_ref[0, slot, i]]
             return carry
 
         lax.fori_loop(0, cap, take_col, 0)
@@ -310,7 +322,7 @@
             device_id={"tile": tile_peer(slot)}, device_id_type=MESH)
 
     def own_col(i, carry):
-        arr[reach][i] = ens_v[pick_ref[reach * cap + i]]
+        arr[reach][i] = ens_v[pick_ref[0, reach, i]]
         return carry
 
     lax.fori_loop(0, cap, own_col, 0)
@@ -354,12 +366,42 @@
         lax.fori_loop(0, share, own, 0)
         waiting.start()
 
+    channels = chans * part
+    group = vec_ref.shape[1]
+    shape = (channels, channels)
+    same = (
+        lax.broadcasted_iota(jnp.int32, shape, 0) // group == lax.broadcasted_iota(jnp.int32, shape, 1) // group
+    )
+    tiled = jnp.concatenate([vec_ref[...]] * (channels // group), 1)
+    basis = jnp.where(same, tiled, 0.0) / jnp.sqrt(val_ref[...])
+    basis_ref[...] = basis
+    turned = basis.T
+    high = turned.astype(jnp.bfloat16)
+    high_ref[...] = high
+    low_ref[...] = (turned - high.astype(jnp.float32)).astype(jnp.bfloat16)
+    innov_v[...] = jnp.dot(
+        innov_ref[...],
+        basis_ref[pl.ds(pl.multiple_of(chan * part, 8), part), :],
+        precision=lax.Precision.HIGHEST,
+        preferred_element_type=jnp.float32,
+    )
+
+    def take_misfit(i, carry):
+        for z in range(chans):
+            misfit_ref[z, pl.ds(i, 1), :] = innov_v[pl.ds(order_ref[z * rows + i], 1), :]
+        return carry
+
+    lax.fori_loop(0, rows, take_misfit, 0)
+
     sequence = sorted(range(chunks), key=lambda q: max(abs(q - reach), abs(q + 1 - reach)))
     half = len(sequence) // 2
     for q in sequence[:half]:
         send_chunk(q)
 
-    for copy in mis_copies + jac_copies:
+    mis_land[chan] = misfit_ref[chan]
+    for copy in mis_copies:
+        copy.start()
+    for copy in jac_copies + mis_copies:
         copy.wait_recv()
     total = mis_land[0]
     for z in range(1, chans):
@@ -382,7 +424,6 @@
 
     gram_ref[...] = jnp.zeros_like(gram_ref)
     pull_ref[...] = jnp.zeros_like(pull_ref)
-    channels = chans * part
     pair = 2 if share % 2 == 0 else 1
 
     for q in sequence:
@@ -413,6 +454,15 @@
         lax.fori_loop(0, share // pair, add, 0)
     for copy in mis_copies + jac_copies + list(tile_copies.values()) + list(col_copies.values()):
         copy.wait_send()
+    half = members // 2
+    parts_ref[:half, :] = gram_ref[:half, :half]
+    parts_ref[half : 2 * half, :] = gram_ref[:half, half:]
+    parts_ref[2 * half : 3 * half, :] = gram_ref[half:, half:]
+    parts_ref[3 * half :, :] = jnp.zeros((parts_ref.shape[0] - 3 * half, half), jnp.float32)
+    pull = pull_ref[0:1, :] + pull_ref[1:2, :]
+    parts_ref[3 * half : 3 * half + 1, :] = pull[:, :half]
+    parts_ref[3 * half + 1 : 3 * half + 2, :] = pull[:, half:]
+    sum_kernel(piece, parts_ref, sums_ref, *sum_refs)
 
 
 def fits(ensemble, jacobian, column_pick, footprint_slot):
@@ -450,28 +500,26 @@
     order = jnp.sum(jnp.where(match, place[None, :], 0), axis=1)
     slots = jnp.sum(jnp.where(match, footprint_slot[None, :], 0), axis=1)
     live = (order < footprint_count[0]).astype(jnp.float32)
-    spread = jnp.tile(error_vectors, (1, channels // group))
-    group_of = jnp.arange(channels) // group
-    basis = jnp.where(group_of[:, None] == group_of[None, :], spread, 0.0) / jnp.sqrt(error_values)[None, :]
-    turned = basis.T
-    high = turned.astype(jnp.bfloat16)
-    low = (turned - high.astype(jnp.float32)).astype(jnp.bfloat16)
-    ours = lax.dynamic_slice_in_dim(basis, chan * part, part, 0)
-    misfit = jnp.dot(innovation, ours, precision=lax.Precision.HIGHEST)
-    misfit = jnp.dot(match.astype(jnp.float32), misfit, precision=lax.Precision.HIGHEST)
-    misfit = misfit.reshape(chans, rows, channels)
+    tiles = lax.axis_size("tile")
+    piece = piece_rows(tiles, members // 2)
+    sums = (piece * tiles, members // 2)
     vmem = pl.BlockSpec(memory_space=pltpu.VMEM)
     smem = pl.BlockSpec(memory_space=pltpu.SMEM)
     half = jnp.bfloat16
-    gram, pull = pl.pallas_call(
-        functools.partial(exchange_kernel, window, cap, chunks, share),
-        out_shape=(
-            jax.ShapeDtypeStruct((members, members), jnp.float32),
-            jax.ShapeDtypeStruct((8, members), jnp.float32),
-        ),
-        in_specs=[smem] * 4 + [pl.BlockSpec(memory_space=pl.ANY)] + [vmem] * 4,
-        out_specs=(vmem, vmem),
+    return pl.pallas_call(
+        functools.partial(exchange_kernel, window, cap, chunks, share, piece),
+        out_shape=jax.ShapeDtypeStruct(sums, jnp.float32),
+        in_specs=[smem] * 4 + [pl.BlockSpec(memory_space=pltpu.HBM)] + [vmem] * 4,
+        out_specs=vmem,
         scratch_shapes=[
+            pltpu.VMEM((members, members), jnp.float32),
+            pltpu.VMEM((8, members), jnp.float32),
+            pltpu.VMEM(sums, jnp.float32),
+            pltpu.VMEM((channels, channels), jnp.float32),
+            pltpu.VMEM((channels, channels), half),
+            pltpu.VMEM((channels, channels), half),
+            pltpu.VMEM((foot_rows, channels), jnp.float32),
+            pltpu.VMEM((chans, rows, channels), jnp.float32),
             pltpu.VMEM(ensemble.shape, half),
             pltpu.VMEM((chans, rows, part, levels), half),
             pltpu.VMEM((chans, rows, part, levels), half),
@@ -487,13 +535,13 @@
             pltpu.SemaphoreType.DMA((2, chans)),
             pltpu.SemaphoreType.DMA((2, chans)),
             pltpu.SemaphoreType.DMA((2, chunks, chans)),
+            *sum_scratch(tiles, chans, piece, members // 2),
         ],
         compiler_params=pltpu.CompilerParams(
             collective_id=1, has_side_effects=True, vmem_limit_bytes=48 * 1024 * 1024
         ),
         name="exchange",
-    )(column_pick.reshape(-1), order, slots, live, ensemble, jacobian, misfit, high, low)
-    return gram, pull[0] + pull[1]
+    )(column_pick, order, slots, live, ensemble, jacobian, innovation, error_vectors, error_values.reshape(1, -1))
 
 
 def from_behind(value, axis, steps):
@@ -565,7 +613,7 @@
     gram_sum = lax.dot_general(
         rounded, rounded, (((0,), (0,)), ((), ())), preferred_element_type=jnp.float32
     )
-    return gram_sum, pull_sum
+    return sum_all(gram_sum, pull_sum)
 
 
 def local(
@@ -581,10 +629,9 @@
 ):
     members = ensemble.shape[2]
     route = exchange if fits(ensemble, jacobian, column_pick, footprint_slot) else exchange_plain
-    gram_sum, pull_sum = route(
+    sums = route(
         ensemble, jacobian, innovation, error_vectors, error_values, column_pick, footprint_slot, footprint_count
     )
-    sums = sum_all(gram_sum, pull_sum)
     updated = finish(sums, ensemble_vectors, ensemble.reshape(-1, members))
     return updated.reshape(ensemble.shape)
 

time: 137 us -> 136 us (level)
  Pallas kernels: 124 us -> 129 us
  other arithmetic: 5.04 us -> 1.88 us
  local copies, waits for them, and re-layouts: 5.87 us -> 4.33 us
    pallas_call x1, Pallas kernels: 94 us -> 117 us  [exchange(): pl.pallas_call(functools.partial(exchange_kernel, window, cap, chunks, sh...]
    pallas_call x1 -> x0, Pallas kernels: 18.4 us -> none  [sum_all(): pl.pallas_call(functools.partial(sum_kernel, piece), out_shape=jax.ShapeD...]
    unnamed x10 -> x11, local copies, waits for them, and re-layouts: 5.04 us -> 4.33 us
where the time goes in v4:
time: 136 us
  Pallas kernels  129 us (95%)
  local copies, waits for them, and re-layouts  4.33 us (3%)
  other arithmetic  1.88 us (1%)
    pallas_call x1, Pallas kernels, exchange(): pl.pallas_call(functools.partial(exchange_kernel, window, cap, chunks, sh...  117 us
    pallas_call x1, Pallas kernels, finish(): pl.pallas_call(functools.partial(finish_kernel, pieces), out_shape=jax.Sh...  11.7 us
    unnamed x11, local copies, waits for them, and re-layouts  4.33 us

profile of v4, /device:TPU:0, one launch (start us, length us, event | category | flops | bytes accessed | tf_op | source)
XLA Modules:
  0.0 135.5 jit_solution(478509291260672603)
XLA Ops:
  0.7 0.9 convert_reduce_fusion
  1.6 0.9 fusion.1
  2.5 0.7 copy.13.pick_ref
  3.2 0.8 copy.15.vec_ref
  4.0 0.9 copy.14.innov_ref
  4.9 0.0 copy-start.1
  4.9 1.3 copy-done.1
  6.2 0.0 copy-start.3
  6.2 0.7 copy-done.3
  6.9 0.0 copy-start
  6.9 0.0 copy-start.2
  6.9 116.9 %exchange.1.sum_ref = f32[448,128]{1,0:T(8,128)S(1)} custom-call(s32[1,5,40]{2,1,0:T(8,128)S(1)} %copy.13.pick_ref, s32[160]{0:T(256)S(1)} %get-tuple-element.6.order_ref, s32[160]{0:T(256)S(1)} %get-tuple-element.5.slot_ref, f32[160]{0:T(256)S(1)} %compare_convert_fusion.live_ref, bf16[384,32,256]{2,1,0:T(8,128)(2,1)} %ens_ref.1, ...), custom_call_target="tpu_custom_call" | custom-call | tf_op jit(solution)/shard_map/exchange/pallas_call | solution.py:509
  123.8 0.0 copy-done
  123.8 0.0 copy-done.2
  123.8 11.7 %finish.1 = bf16[12288,256]{1,0:T(8,128)(2,1)} custom-call(f32[448,128]{1,0:T(8,128)S(1)} %exchange.1.sum_ref, f32[256,256]{1,0:T(8,128)S(1)} %copy-done.2, bf16[12288,256]{1,0:T(8,128)(2,1)S(1)} %bitcast.5), custom_call_target="tpu_custom_call" | custom-call | tf_op jit(solution)/shard_map/finish/pallas_call | solution.py:228
  (2 shorter events, 0.0 us)
Async XLA Ops:
  4.9 1.3 copy-start.1
  6.2 0.7 copy-start.3
  6.9 116.9 %copy-start = (bf16[384,32,256]{2,1,0:T(8,128)(2,1)S(1)}, bf16[384,32,256]{2,1,0:T(8,128)(2,1)}, u32[]{:S(2)}) copy-start(bf16[384,32,256]{2,1,0:T(8,128)(2,1)} %ens_ref.1) | copy-start | bytes 18874372
  6.9 116.9 %copy-start.2 = (f32[256,256]{1,0:T(8,128)S(1)}, f32[256,256]{1,0:T(8,128)}, u32[]{:S(2)}) copy-start(f32[256,256]{1,0:T(8,128)} %vec_ref.2) | copy-start | bytes 786436

commit v5 on v4

--- a/solution.py
+++ b/solution.py
@@ -367,21 +367,22 @@
         waiting.start()
 
     channels = chans * part
-    group = vec_ref.shape[1]
+    group = vec_ref.shape[0]
     shape = (channels, channels)
     same = (
         lax.broadcasted_iota(jnp.int32, shape, 0) // group == lax.broadcasted_iota(jnp.int32, shape, 1) // group
     )
-    tiled = jnp.concatenate([vec_ref[...]] * (channels // group), 1)
+    tiled = jnp.concatenate([vec_ref[...]] * (channels // group), 0).T
     basis = jnp.where(same, tiled, 0.0) / jnp.sqrt(val_ref[...])
     basis_ref[...] = basis
     turned = basis.T
     high = turned.astype(jnp.bfloat16)
     high_ref[...] = high
     low_ref[...] = (turned - high.astype(jnp.float32)).astype(jnp.bfloat16)
-    innov_v[...] = jnp.dot(
+    innov_v[...] = lax.dot_general(
         innov_ref[...],
         basis_ref[pl.ds(pl.multiple_of(chan * part, 8), part), :],
+        (((0,), (0,)), ((), ())),
         precision=lax.Precision.HIGHEST,
         preferred_element_type=jnp.float32,
     )
@@ -392,21 +393,17 @@
         return carry
 
     lax.fori_loop(0, rows, take_misfit, 0)
+    mis_land[chan] = misfit_ref[chan]
+    for copy in mis_copies:
+        copy.start()
 
     sequence = sorted(range(chunks), key=lambda q: max(abs(q - reach), abs(q + 1 - reach)))
     half = len(sequence) // 2
     for q in sequence[:half]:
         send_chunk(q)
 
-    mis_land[chan] = misfit_ref[chan]
-    for copy in mis_copies:
-        copy.start()
-    for copy in jac_copies + mis_copies:
+    for copy in jac_copies:
         copy.wait_recv()
-    total = mis_land[0]
-    for z in range(1, chans):
-        total = total + mis_land[z]
-    mis_all[...] = total
 
     def whiten(i, carry):
         block = jac_land[:, i].reshape(chans * part, levels)
@@ -421,6 +418,12 @@
     lax.fori_loop(0, rows, whiten, 0)
     for q in sequence[half:]:
         send_chunk(q)
+    for copy in mis_copies:
+        copy.wait_recv()
+    total = mis_land[0]
+    for z in range(1, chans):
+        total = total + mis_land[z]
+    mis_all[...] = total
 
     gram_ref[...] = jnp.zeros_like(gram_ref)
     pull_ref[...] = jnp.zeros_like(pull_ref)
@@ -541,7 +544,7 @@
             collective_id=1, has_side_effects=True, vmem_limit_bytes=48 * 1024 * 1024
         ),
         name="exchange",
-    )(column_pick, order, slots, live, ensemble, jacobian, innovation, error_vectors, error_values.reshape(1, -1))
+    )(column_pick, order, slots, live, ensemble, jacobian, innovation.T, error_vectors.T, error_values.reshape(1, -1))
 
 
 def from_behind(value, axis, steps):

time: 136 us -> 127 us (0.934)
  Pallas kernels: 129 us -> 120 us
    pallas_call x1, Pallas kernels: 117 us -> 108 us  [exchange(): pl.pallas_call(functools.partial(exchange_kernel, window, cap, chunks, sh...]
    unnamed x11 -> x13, local copies, waits for them, and re-layouts: 4.33 us -> 4.14 us
where the time goes in v5:
time: 127 us
  Pallas kernels  120 us (94%)
  local copies, waits for them, and re-layouts  4.14 us (3%)
  other arithmetic  1.96 us (2%)
    pallas_call x1, Pallas kernels, exchange(): pl.pallas_call(functools.partial(exchange_kernel, window, cap, chunks, sh...  108 us
    pallas_call x1, Pallas kernels, finish(): pl.pallas_call(functools.partial(finish_kernel, pieces), out_shape=jax.Sh...  11.7 us
    unnamed x13, local copies, waits for them, and re-layouts  4.14 us

profile of v5, /device:TPU:0, one launch (start us, length us, event | category | flops | bytes accessed | tf_op | source)
XLA Modules:
  0.0 127.1 jit_solution(12585668739860838070)
XLA Ops:
  0.0 0.0 copy-start
  0.8 1.0 convert_reduce_fusion
  1.9 0.9 fusion.1
  2.8 0.7 copy.11.pick_ref
  3.5 0.0 copy-start.1
  3.5 1.3 %copy-done.1 = bf16[160,32,128]{2,1,0:T(8,128)(2,1)S(1)} copy-done((bf16[160,32,128]{2,1,0:T(8,128)(2,1)S(1)}, bf16[160,32,128]{2,1,0:T(8,128)(2,1)}, u32[]{:S(2)}) %copy-start.1) | copy-done | bytes 1310744
  4.8 0.0 copy-start.3
  4.8 0.8 copy-done.3
  5.5 0.0 copy-start.4
  5.5 0.7 copy-done.4
  6.3 0.0 copy-start.5
  6.3 0.7 copy-done.5
  6.9 0.0 copy-start.2
  6.9 108.5 %exchange.1.sum_ref = f32[448,128]{1,0:T(8,128)S(1)} custom-call(s32[1,5,40]{2,1,0:T(8,128)S(1)} %copy.11.pick_ref, s32[160]{0:T(256)S(1)} %get-tuple-element.6.order_ref, s32[160]{0:T(256)S(1)} %get-tuple-element.5.slot_ref, f32[160]{0:T(256)S(1)} %compare_convert_fusion.live_ref, bf16[384,32,256]{2,1,0:T(8,128)(2,1)} %ens_ref.1, ...), custom_call_target="tpu_custom_call" | custom-call | tf_op jit(solution)/shard_map/exchange/pallas_call | solution.py:512
  115.4 0.0 copy-done
  115.4 0.0 copy-done.2
  115.4 11.7 %finish.1 = bf16[12288,256]{1,0:T(8,128)(2,1)} custom-call(f32[448,128]{1,0:T(8,128)S(1)} %exchange.1.sum_ref, f32[256,256]{1,0:T(8,128)S(1)} %copy-done.2, bf16[12288,256]{1,0:T(8,128)(2,1)S(1)} %bitcast.7), custom_call_target="tpu_custom_call" | custom-call | tf_op jit(solution)/shard_map/finish/pallas_call | solution.py:228
  (2 shorter events, 0.0 us)
Async XLA Ops:
  0.0 115.4 %copy-start = (bf16[384,32,256]{2,1,0:T(8,128)(2,1)S(1)}, bf16[384,32,256]{2,1,0:T(8,128)(2,1)}, u32[]{:S(2)}) copy-start(bf16[384,32,256]{2,1,0:T(8,128)(2,1)} %ens_ref.1) | copy-start | bytes 18874372
  3.5 1.3 %copy-start.1 = (bf16[160,32,128]{2,1,0:T(8,128)(2,1)S(1)}, bf16[160,32,128]{2,1,0:T(8,128)(2,1)}, u32[]{:S(2)}) copy-start(bf16[160,32,128]{2,1,0:T(8,128)(2,1)} %jac_ref.1) | copy-start | bytes 3932164
  4.8 0.8 copy-start.3
  5.5 0.7 copy-start.4
  6.3 0.7 copy-start.5
  6.9 108.5 %copy-start.2 = (f32[256,256]{1,0:T(8,128)S(1)}, f32[256,256]{1,0:T(8,128)}, u32[]{:S(2)}) copy-start(f32[256,256]{1,0:T(8,128)} %vec_ref.1) | copy-start | bytes 786436
